TPU v7x, 32 devices: a whole 2x2x4 slice. The times are simulated.
32 devices in a mesh: segment: 2 (over core), expert: 4 (over z), tensor: 4 (over y, x).
Axes of the slice: x: 2, y: 2, z: 4, core: 2. Of those that a mesh axis runs over, the one named last changes fastest.
Arguments:
- activations: bfloat16 [2, 256, 2560], P('segment', 'expert', 'tensor'), may hold values from -48 to 48
- expert_ids: int32 [2, 256, 6], P(None, 'expert'), may hold values from 0 to 7, as said below
- route_weights: float32 [2, 256, 6], P(None, 'expert'), may hold values from 0.05 to 1
- gain_dense: float32 [2560], replicated, may hold values from 0.25 to 1.75
- gain_expert: float32 [2560], replicated, may hold values from 0.25 to 1.75
- dense_gate: bfloat16 [2560, 6144], P('expert', 'tensor'), may hold values from -0.125 to 0.125
- dense_up: bfloat16 [2560, 6144], P('expert', 'tensor'), may hold values from -0.125 to 0.125
- dense_down: bfloat16 [2560, 6144], P('expert', 'tensor'), may hold values from -0.078125 to 0.078125
- expert_gate: bfloat16 [8, 2560, 1536], P('expert', None, 'tensor'), may hold values from -0.125 to 0.125
- expert_up: bfloat16 [8, 2560, 1536], P('expert', None, 'tensor'), may hold values from -0.125 to 0.125
- expert_down: bfloat16 [8, 1536, 2560], P('expert', 'tensor'), may hold values from -0.15625 to 0.15625
Outputs:
- sections: bfloat16 [2, 2, 256, 2560], P('segment', None, 'expert', 'tensor')
Inputs may be any that keep to these rules, and one draw needn't show every extreme that they name: `expert_ids`: each token names 6 different experts. Split each micro-batch's tokens into blocks of 64 in order: no expert is named by more than 64 tokens of one block, and in every micro-batch one expert is named by exactly 64 tokens of every block.
All inputs are finite; a program needn't handle non-finite values.
Results may differ from a plain program's by a relative error of at most 0.009.
Values may be sent and summed in bfloat16 or wider, within the bound.
No kernel may reach another device: no remote copies, remote signals or barrier semaphores. Data moves between devices by JAX's collectives and lax.ppermute only.
A program may use at most 128 MiB of HBM per device.

v0:
```python
import jax
import jax.numpy as jnp
from jax import lax
from jax.sharding import PartitionSpec as P

EPSILON = 1e-06


def shifted(block, axis, distance):
    devices = range(lax.axis_size(axis))
    route = [((i - distance) % len(devices), i) for i in devices]
    return lax.ppermute(block, axis, route)


def normalize(values, gain_row):
    inverse = lax.rsqrt(jnp.mean(values * values, axis=-1, keepdims=True) + EPSILON)
    return values * inverse * gain_row


def dense_prepare(micro_block, gain_dense):
    micro_count, tokens_here, quarter = micro_block.shape
    whole_rows = lax.all_gather(micro_block, "tensor", axis=2, tiled=True)
    full_width = whole_rows.shape[2]
    normed = normalize(whole_rows.astype(jnp.float32), gain_dense).astype(jnp.bfloat16)
    return normed.reshape(micro_count * tokens_here, full_width)


def dense_finish(micro_block, partial_value):
    micro_count, tokens_here, quarter = micro_block.shape
    summed = lax.psum_scatter(
        partial_value.reshape(micro_count, tokens_here, partial_value.shape[1]).astype(
            jnp.bfloat16
        ),
        "tensor",
        scatter_dimension=2,
        tiled=True,
    ).astype(jnp.float32)
    return (micro_block.astype(jnp.float32) + summed).astype(jnp.bfloat16)


def dense_folded(activations, gain_dense, dense_gate, dense_up, dense_down):
    normed = dense_prepare(activations, gain_dense)
    gate_sums = jnp.dot(
        normed,
        lax.all_gather(dense_gate, "expert", axis=0, tiled=True),
        preferred_element_type=jnp.float32,
    )
    upward = jnp.dot(
        normed,
        lax.all_gather(dense_up, "expert", axis=0, tiled=True),
        preferred_element_type=jnp.float32,
    )
    hidden = (jax.nn.silu(gate_sums) * upward).astype(jnp.bfloat16)
    partial_value = lax.dot_general(
        hidden,
        lax.all_gather(dense_down, "expert", axis=0, tiled=True),
        (((1,), (1,)), ((), ())),
        preferred_element_type=jnp.float32,
    )
    return dense_finish(activations, partial_value)


def route_slots(expert_ids_block, local_count, groups, capacity):
    tokens_here, picks = expert_ids_block.shape
    flat_ids = expert_ids_block.reshape(-1)
    experts_all = local_count * groups
    one_hot = (flat_ids[:, None] == jnp.arange(experts_all, dtype=jnp.int32)[None, :]).astype(
        jnp.int32
    )
    ranks = jnp.sum((jnp.cumsum(one_hot, axis=0) - 1) * one_hot, axis=1)
    slots = (flat_ids % local_count * groups + flat_ids // local_count) * capacity + ranks
    owners = jnp.arange(tokens_here * picks, dtype=jnp.int32) // picks
    sources = jnp.full((experts_all * capacity,), tokens_here, jnp.int32).at[slots].set(owners)
    return (slots, sources)


def place_rows(normed, sources, local_count, groups, capacity):
    padded = jnp.concatenate([normed, jnp.zeros((1, normed.shape[1]), normed.dtype)], axis=0)
    return padded[sources].reshape(local_count, groups, capacity, normed.shape[1])


def expert_block(
    middle, expert_ids_block, route_block, gain_expert, expert_gate, expert_up, expert_down
):
    tokens_here, quarter = middle.shape
    picks = expert_ids_block.shape[1]
    groups = lax.axis_size("expert")
    local_count, full_width, hidden_part = expert_gate.shape
    capacity = min(tokens_here, 2 * (tokens_here * picks // (local_count * groups)))
    slots, sources = route_slots(expert_ids_block, local_count, groups, capacity)
    middle_wide = middle.astype(jnp.float32)
    received_rows = groups * capacity
    tensor_index = lax.axis_index("tensor")
    square_sums = lax.psum(jnp.sum(middle_wide * middle_wide, axis=1), "tensor")
    inverse = lax.rsqrt(square_sums / full_width + EPSILON)
    gain_part = lax.dynamic_slice_in_dim(gain_expert, tensor_index * quarter, quarter, 0)
    normed = (middle_wide * inverse[:, None] * gain_part).astype(jnp.bfloat16)
    outgoing = place_rows(normed, sources, local_count, groups, capacity)
    arrived = lax.all_to_all(outgoing, "expert", split_axis=1, concat_axis=1, tiled=True)
    arrived = arrived.reshape(local_count, received_rows, quarter)
    slice_part = lax.all_gather(arrived, "tensor", axis=2, tiled=True)
    gate_sums = jnp.einsum(
        "lrc,lch->lrh", slice_part, expert_gate, preferred_element_type=jnp.float32
    )
    upward = jnp.einsum("lrc,lch->lrh", slice_part, expert_up, preferred_element_type=jnp.float32)
    hidden = (jax.nn.silu(gate_sums) * upward).astype(jnp.bfloat16)
    partial_value = jnp.einsum(
        "lrh,lhd->lrd", hidden, expert_down, preferred_element_type=jnp.float32
    )
    summed = lax.psum_scatter(
        partial_value.astype(jnp.bfloat16), "tensor", scatter_dimension=2, tiled=True
    )
    returned = lax.all_to_all(
        summed.reshape(local_count, groups, capacity, quarter),
        "expert",
        split_axis=1,
        concat_axis=1,
        tiled=True,
    )
    picked = returned.reshape(local_count * groups * capacity, quarter)[slots]
    picked = picked.reshape(tokens_here, picks, quarter).astype(jnp.float32)
    mixed = jnp.sum(route_block[:, :, None] * picked, axis=1)
    return (middle_wide + mixed).astype(jnp.bfloat16)


def body(
    activations,
    expert_ids,
    route_weights,
    gain_dense,
    gain_expert,
    dense_gate,
    dense_up,
    dense_down,
    expert_gate,
    expert_up,
    expert_down,
):
    segment_index = lax.axis_index("segment")
    own_middle = dense_folded(activations, gain_dense, dense_gate, dense_up, dense_down)
    other_middle = shifted(own_middle, "segment", 1)
    middles = jnp.where(
        segment_index == 0,
        jnp.concatenate([own_middle, other_middle], axis=0),
        jnp.concatenate([other_middle, own_middle], axis=0),
    )
    finals = jnp.stack(
        [
            expert_block(
                middles[position],
                expert_ids[position],
                route_weights[position],
                gain_expert,
                expert_gate,
                expert_up,
                expert_down,
            )
            for position in range(middles.shape[0])
        ]
    )
    sections = jnp.where(segment_index == 0, middles, finals)
    return sections[None]


def solution(mesh):
    placed = (
        P("segment", "expert", "tensor"),
        P(None, "expert", None),
        P(None, "expert", None),
        P(),
        P(),
        P("expert", "tensor"),
        P("expert", "tensor"),
        P("expert", "tensor"),
        P("expert", None, "tensor"),
        P("expert", None, "tensor"),
        P("expert", "tensor", None),
    )
    return jax.shard_map(
        body,
        mesh=mesh,
        in_specs=placed,
        out_specs=P("segment", None, "expert", "tensor"),
        check_vma=False,
    )
```

profile of v0, /device:TPU:0, one launch (start us, length us, event | category | flops | bytes accessed | tf_op | source)
XLA Modules:
  0.0 708.2 jit_solution(15755133042665731109)
XLA Ops:
  10.2 11.0 %all_gather.18 = bf16[1,64,2560]{2,1,0:T(8,128)(2,1)S(1)} all-gather(bf16[1,64,640]{2,1,0:T(8,128)(2,1)S(1)} %copy-done.4), channel_id=1, replica_groups=mesh['segment'=2,'expert'=4,'tensor'=4] {'tensor'}, dimensions={2}, use_global_device_ids=true | all-gather | bytes 409600 | tf_op jit(solution)/shard_map/all_gather | solution.py:22
  21.4 131.3 %all-gather.6.cloned.1.call-done = bf16[2560,1536]{1,0:T(8,128)(2,1)} async-done(((bf16[640,1536]{1,0:T(8,128)(2,1)}), bf16[2560,1536]{1,0:T(8,128)(2,1)}) %all-gather.6.cloned.1.call-update) | async-done | bytes 7864336 | tf_op jit(solution)/shard_map/all_gather | solution.py:45
  152.7 4.8 fusion.41
  157.5 136.1 %all-gather.10.cloned.1.call-done = bf16[2560,1536]{1,0:T(8,128)(2,1)} async-done(((bf16[640,1536]{1,0:T(8,128)(2,1)}), bf16[2560,1536]{1,0:T(8,128)(2,1)}) %all-gather.10.cloned.1.call-update) | async-done | bytes 7864336 | tf_op jit(solution)/shard_map/all_gather | solution.py:56
  293.5 140.8 %all-gather.8.cloned.1.call-done = bf16[2560,1536]{1,0:T(8,128)(2,1)} async-done(((bf16[640,1536]{1,0:T(8,128)(2,1)}), bf16[2560,1536]{1,0:T(8,128)(2,1)}) %all-gather.8.cloned.1.call-update) | async-done | bytes 7864336 | tf_op jit(solution)/shard_map/all_gather | solution.py:50
  434.4 9.4 %fusion = bf16[1,64,2560]{2,1,0:T(8,128)(2,1)S(1)} fusion(bf16[2560,1536]{1,0:T(8,128)(2,1)} %all-gather.10.cloned.1.call-done, bf16[2560,1536]{1,0:T(8,128)(2,1)} %all-gather.8.cloned.1.call-done, f32[64,1536]{1,0:T(8,128)S(1)} %fusion.41, bf16[1,64,2560]{2,1,0:T(8,128)(2,1)S(1)} %all_gather.18, f32[2560]{0:T(1024)S(1)} %copy-done.5, f32[64]{0:T(128)S(1)} %add_rsqrt_fusion.2), kind=kOutput, calls=%fused_computation.9 | convolution fusion | flops 1008041984 | bytes 16787712 | tf_op jit(solution)/shard_map/dot_general | solution.py:54
  446.9 2.9 scatter_custom_fusion.1
  449.8 19.9 %reduce-scatter.10.cloned.1.call-done = bf16[640,64]{1,0:T(8,128)(2,1)} async-done(((bf16[2560,64]{1,0:T(8,128)(2,1)}), bf16[640,64]{1,0:T(8,128)(2,1)}) %reduce-scatter.10.cloned.1.call-update) | async-done | bytes 81936
  473.1 8.9 %all-reduce.2 = (f32[64]{0:T(128)S(1)}, f32[64]{0:T(128)S(1)}) all-reduce(f32[64]{0:T(128)S(1)} %get-tuple-element.5, f32[64]{0:T(128)S(1)} %get-tuple-element.6), channel_id=1, replica_groups=mesh['segment'=2,'expert'=4,'tensor'=4] {'tensor'}, use_global_device_ids=true, to_apply=%region_3.4 | all-reduce | flops 128 | bytes 1024 | tf_op jit(solution)/shard_map/psum | solution.py:94
  482.2 2.0 gather_fusion.2
  484.3 20.0 %all_to_all.20 = bf16[2,4,64,640]{3,2,0,1:T(8,128)(2,1)S(1)} all-to-all(bf16[2,4,64,640]{3,2,0,1:T(8,128)(2,1)S(1)} %copy.38), channel_id=1, replica_groups=mesh['segment'=2,'expert'=4,'tensor'=4] {'expert'}, dimensions={1} | all-to-all | bytes 1310720 | tf_op jit(solution)/shard_map/all_to_all | solution.py:99
  507.0 2.9 scatter_custom_fusion
  510.0 2.0 gather_fusion
  512.1 18.8 %all_to_all.21 = bf16[2,4,64,640]{3,2,0,1:T(8,128)(2,1)S(1)} all-to-all(bf16[2,4,64,640]{3,2,0,1:T(8,128)(2,1)S(1)} %copy.29), channel_id=1, replica_groups=mesh['segment'=2,'expert'=4,'tensor'=4] {'expert'}, dimensions={1} | all-to-all | bytes 1310720 | tf_op jit(solution)/shard_map/all_to_all | solution.py:99
  532.0 11.0 %all-gather.14.cloned.1.call-done = bf16[2,256,2560]{2,1,0:T(8,128)(2,1)} async-done(((bf16[2,256,640]{2,1,0:T(8,128)(2,1)}), bf16[2,256,2560]{2,1,0:T(8,128)(2,1)}) %all-gather.14.cloned.1.call-update) | async-done | bytes 2621456 | tf_op jit(solution)/shard_map/all_gather | solution.py:101
  543.0 5.5 fusion.68
  548.5 8.2 %convolution_convert_fusion = bf16[2,256,2560]{2,1,0:T(8,128)(2,1)} fusion(bf16[2,384,2560]{2,1,0:T(8,128)(2,1)} %param.21, bf16[2,256,2560]{2,1,0:T(8,128)(2,1)S(1)} %copy-done, bf16[2,2560,384]{2,1,0:T(8,128)(2,1)} %param.20, f32[2,256,384]{2,1,0:T(8,128)} %fusion.68), kind=kOutput, calls=%fused_computation.6 | convolution fusion | flops 2015756288 | bytes 13893632 | tf_op jit(solution)/shard_map/lrh,lhd->lrd/dot_general | solution.py:107
  556.7 6.0 copy.46
  562.7 2.0 copy.54
  564.7 19.5 %all-gather.12.cloned.1.call-done = bf16[2,256,2560]{2,1,0:T(8,128)(2,1)} async-done(((bf16[2,256,640]{2,1,0:T(8,128)(2,1)}), bf16[2,256,2560]{2,1,0:T(8,128)(2,1)}) %all-gather.12.cloned.1.call-update) | async-done | bytes 2621456 | tf_op jit(solution)/shard_map/all_gather | solution.py:101
  584.2 5.5 fusion.67
  589.7 8.0 %convolution_convert_fusion.1 = bf16[2,256,2560]{2,1,0:T(8,128)(2,1)} fusion(bf16[2,384,2560]{2,1,0:T(8,128)(2,1)} %param.21, bf16[2,256,2560]{2,1,0:T(8,128)(2,1)S(1)} %copy-done.1, bf16[2,2560,384]{2,1,0:T(8,128)(2,1)} %param.20, f32[2,256,384]{2,1,0:T(8,128)} %fusion.67), kind=kOutput, calls=%fused_computation.7 | convolution fusion | flops 2015756288 | bytes 13893632 | tf_op jit(solution)/shard_map/lrh,lhd->lrd/dot_general | solution.py:107
  597.7 6.0 copy.44
  605.7 21.1 %reduce-scatter.14.cloned.1.call-done = bf16[640,512]{1,0:T(8,128)(2,1)} async-done(((bf16[2560,512]{1,0:T(8,128)(2,1)}), bf16[640,512]{1,0:T(8,128)(2,1)}) %reduce-scatter.14.cloned.1.call-update) | async-done | bytes 655376
  626.8 2.0 reshape.494
  630.7 4.6 all-to-all-start.3
  635.3 34.1 %reduce-scatter.12.cloned.1.call-done = bf16[640,512]{1,0:T(8,128)(2,1)} async-done(((bf16[2560,512]{1,0:T(8,128)(2,1)}), bf16[640,512]{1,0:T(8,128)(2,1)}) %reduce-scatter.12.cloned.1.call-update) | async-done | bytes 655376
  669.4 2.0 reshape.492
  673.3 4.6 all-to-all-start.1
  678.8 2.2 gather_fusion.3
  681.1 13.9 %all-to-all-done.1 = bf16[2,4,64,640]{3,2,0,1:T(8,128)(2,1)S(1)} async-done(((bf16[2,4,64,640]{3,2,0,1:T(8,128)(2,1)}), bf16[2,4,64,640]{3,2,0,1:T(8,128)(2,1)S(1)}, u32[]{:S(2)}, u32[]{:S(2)}) %all-to-all-start.1) | async-done | bytes 655392 | tf_op jit(solution)/shard_map/all_to_all | solution.py:113
  695.1 2.6 gather_fusion.1
  (97 shorter events, 24.8 us)
Async XLA Ops:
  6.5 2.3 copy-start.6
  6.5 3.7 copy-start.4
  6.5 146.2 %copy-start.5 = (f32[2560]{0:T(1024)S(1)}, f32[2560]{0:T(1024)}, u32[]{:S(2)}) copy-start(f32[2560]{0:T(1024)} %param.14) | copy-start | bytes 30724
  6.5 146.2 %all-gather.6.cloned.1.call-start = ((), (), s32[]{:S(2)}) async-start(), calls=%async_computation.7 | async-start | bytes 9830400 | tf_op jit(solution)/shard_map/all_gather | solution.py:45
  7.3 286.3 %all-gather.10.cloned.1.call-start = ((), (), s32[]{:S(2)}) async-start(), calls=%async_computation.9 | async-start | bytes 9830400 | tf_op jit(solution)/shard_map/all_gather | solution.py:56
  8.0 426.4 %all-gather.8.cloned.1.call-start = ((), (), s32[]{:S(2)}) async-start(), calls=%async_computation.8 | async-start | bytes 9830400 | tf_op jit(solution)/shard_map/all_gather | solution.py:50
  8.7 460.9 %reduce-scatter.10.cloned.1.call-start = ((), (), s32[]{:S(2)}) async-start(), calls=%async_computation.12 | async-start | bytes 819200
  445.7 97.3 %all-gather.14.cloned.1.call-start = ((), (), s32[]{:S(2)}) async-start(), calls=%async_computation.11 | async-start | bytes 3276800 | tf_op jit(solution)/shard_map/all_gather | solution.py:101
  470.9 1.3 collective-permute-start
  472.3 0.6 copy-start.2
  505.2 79.0 %all-gather.12.cloned.1.call-start = ((), (), s32[]{:S(2)}) async-start(), calls=%async_computation.10 | async-start | bytes 3276800 | tf_op jit(solution)/shard_map/all_gather | solution.py:101
  531.8 95.0 %reduce-scatter.14.cloned.1.call-start = ((), (), s32[]{:S(2)}) async-start(), calls=%async_computation.14 | async-start | bytes 3276800
  543.0 5.5 copy-start
  564.7 104.7 %reduce-scatter.12.cloned.1.call-start = ((), (), s32[]{:S(2)}) async-start(), calls=%async_computation.13 | async-start | bytes 3276800
  584.2 5.5 copy-start.1
  629.8 48.1 %copy-start.7 = (f32[2,64,6]{1,0,2:T(2,128)S(1)}, f32[2,64,6]{1,0,2:T(2,128)}, u32[]{:S(2)}) copy-start(f32[2,64,6]{1,0,2:T(2,128)} %param.13) | copy-start | bytes 9220
  630.7 42.6 %all-to-all-start.3 = ((bf16[2,4,64,640]{3,2,0,1:T(8,128)(2,1)}), bf16[2,4,64,640]{3,2,0,1:T(8,128)(2,1)S(1)}, u32[]{:S(2)}, u32[]{:S(2)}) async-start(bf16[2,4,64,640]{3,2,0,1:T(8,128)(2,1)} %copy.40), calls=%async_computation.3 | async-start | bytes 1310720 | tf_op jit(solution)/shard_map/all_to_all | solution.py:113
  673.3 21.7 %all-to-all-start.1 = ((bf16[2,4,64,640]{3,2,0,1:T(8,128)(2,1)}), bf16[2,4,64,640]{3,2,0,1:T(8,128)(2,1)S(1)}, u32[]{:S(2)}, u32[]{:S(2)}) async-start(bf16[2,4,64,640]{3,2,0,1:T(8,128)(2,1)} %copy.31), calls=%async_computation.1 | async-start | bytes 1310720 | tf_op jit(solution)/shard_map/all_to_all | solution.py:113
  697.7 3.0 copy-start.3
Sparse Core Ops, SparseCore 0:
  8.9 143.7 all-gather.5
  154.3 139.2 all-gather.9
  295.1 139.2 all-gather.7
  445.8 23.8 reduce-scatter.9
  505.3 37.6 all-gather.13
  544.7 39.5 all-gather.11
  587.2 39.5 reduce-scatter.13
  629.8 39.5 reduce-scatter.11
where the time goes:
time: 709 us; the launch traced here: 708 us
  waiting for transfers between devices  531 us (75%)
  blocking collectives  58.7 us (8%)
  local copies, waits for them, and re-layouts  48.6 us (7%)
  matrix products  41.3 us (6%)
  between operations  13.9 us (2%)
  starting transfers between devices  9.73 us (1%)
    all_gather x1, waiting for transfers between devices, dense_folded(): lax.all_gather(dense_up, 'expert', axis=0, tiled=True)  141 us
    all_gather x1, waiting for transfers between devices, dense_folded(): lax.all_gather(dense_down, 'expert', axis=0, tiled=True)  136 us
    all_gather x1, waiting for transfers between devices, dense_folded(): lax.all_gather(dense_gate, 'expert', axis=0, tiled=True)  131 us
    unnamed x11, waiting for transfers between devices  77.2 us
    all_to_all x2, blocking collectives, expert_block(): lax.all_to_all(outgoing, 'expert', split_axis=1, concat_axis=1, tiled=True)  38.8 us
    all_gather x2, waiting for transfers between devices, expert_block(): slice_part = lax.all_gather(arrived, 'tensor', axis=2, tiled=True)  30.5 us
    unnamed x28, local copies, waits for them, and re-layouts  25.6 us
    dot_general x2, matrix products, expert_block(): jnp.einsum('lrh,lhd->lrd', hidden, expert_down, preferred_element_type=jn...  16.2 us
  transfers between devices with their start and end apart: 11, of which 10 were waited for; matrix products, arithmetic and copies ran while one was open for 10% of the time, Pallas kernels for 0%

commit v1 on v0

--- a/solution.py
+++ b/solution.py
@@ -123,7 +123,7 @@
     return (middle_wide + mixed).astype(jnp.bfloat16)
 
 
-def body(
+def general_body(
     activations,
     expert_ids,
     route_weights,
@@ -162,6 +162,154 @@
     return sections[None]
 
 
+def swap(block, axis, distance):
+    devices = range(lax.axis_size(axis))
+    return lax.ppermute(block, axis, [(i, i ^ distance) for i in devices])
+
+
+def transposed(block):
+    size = lax.axis_size("tensor")
+    route = [(a * size + b, b * size + a) for a in range(size) for b in range(size)]
+    return lax.ppermute(block, ("expert", "tensor"), route)
+
+
+def gathered(block, axis):
+    size = lax.axis_size(axis)
+    arrived = {d: swap(block, axis, d) for d in range(size - 1, 0, -1)}
+    return [block] + [arrived[d] for d in range(1, size)]
+
+
+def traded(blocks, axis):
+    size = lax.axis_size(axis)
+    sent = {d: swap(blocks[d].astype(jnp.bfloat16), axis, d) for d in range(size - 1, 0, -1)}
+    total = blocks[0].astype(jnp.float32)
+    for d in range(1, size):
+        total = total + sent[d].astype(jnp.float32)
+    return total
+
+
+def pick(stacked, index):
+    return lax.dynamic_index_in_dim(stacked, index, 0, keepdims=False)
+
+
+def two_parts(values):
+    high = lax.reduce_precision(values, 8, 7)
+    return jnp.concatenate([high, values - high], axis=1).astype(jnp.bfloat16)
+
+
+def padded_columns(values):
+    extra = -values.shape[1] % 128
+    return jnp.pad(values, ((0, 0), (0, extra)))
+
+
+def stream(block, expert_ids, route, gains, weights):
+    gain_dense, gain_expert = gains
+    dense_gate, dense_up, dense_down, expert_gate, expert_up, expert_down = weights
+    size = lax.axis_size("tensor")
+    mine_e, mine_t = lax.axis_index("expert"), lax.axis_index("tensor")
+    rows, part = block.shape
+    full_width = part * size
+    hidden = dense_gate.shape[1]
+    local_count, _, hidden_part = expert_gate.shape
+    expert_total = local_count * size
+
+    turned = transposed(block)
+    arrived = jnp.stack(gathered(turned, "tensor"))
+    gain_block = lax.dynamic_slice_in_dim(gain_dense, mine_e * part, part, 0)
+    across = mine_e ^ mine_t
+    tokens = jnp.concatenate([pick(arrived, d ^ across) for d in range(size)])
+    wide = tokens.astype(jnp.float32)
+    scaled = (wide * gain_block).astype(jnp.bfloat16)
+    squares = two_parts(jnp.sum(wide * wide, axis=1, keepdims=True))
+    partial_sums = jnp.concatenate(
+        [
+            jnp.dot(scaled, dense_gate, preferred_element_type=jnp.float32).astype(jnp.bfloat16),
+            jnp.dot(scaled, dense_up, preferred_element_type=jnp.float32).astype(jnp.bfloat16),
+            padded_columns(squares),
+        ],
+        axis=1,
+    ).reshape(size, rows, -1)
+    sums = traded([partial_sums[d] for d in range(size)], "expert")
+    square_sum = sums[:, 2 * hidden : 2 * hidden + 1] + sums[:, 2 * hidden + 1 : 2 * hidden + 2]
+    inverse = lax.rsqrt(square_sum / full_width + EPSILON)
+    act = jax.nn.silu(sums[:, :hidden] * inverse) * (sums[:, hidden : 2 * hidden] * inverse)
+
+    chosen = expert_ids[:, :, None] == jnp.arange(expert_total, dtype=jnp.int32)
+    shares = jnp.sum(jnp.where(chosen, route[:, :, None], 0.0), axis=1)
+    carried = jnp.concatenate([act.astype(jnp.bfloat16), padded_columns(two_parts(shares))], axis=1)
+    all_carried = jnp.stack(gathered(carried, "expert"))
+    down = lax.dot_general(
+        all_carried[:, :, :hidden].reshape(size * rows, hidden),
+        dense_down,
+        (((1,), (1,)), ((), ())),
+        preferred_element_type=jnp.float32,
+    )
+    down = down.astype(jnp.bfloat16).reshape(size, rows, part)
+    summed = traded([pick(down, d ^ across) for d in range(size)], "tensor")
+    middle_turned = (turned.astype(jnp.float32) + summed).astype(jnp.bfloat16)
+    middle = transposed(middle_turned)
+
+    parts = jnp.stack(gathered(middle_turned, "expert"))
+    row = jnp.concatenate([pick(parts, b ^ mine_e) for b in range(size)], axis=1)
+    normed = normalize(row.astype(jnp.float32), gain_expert).astype(jnp.bfloat16)
+    spread = jnp.concatenate(gathered(normed, "tensor"))
+
+    all_shares = jnp.stack(
+        [pick(all_carried[:, :, hidden:], d ^ across) for d in range(size)]
+    ).reshape(size * rows, -1)
+    all_shares = (
+        all_shares[:, :expert_total].astype(jnp.float32)
+        + all_shares[:, expert_total : 2 * expert_total].astype(jnp.float32)
+    )
+    own_shares = lax.dynamic_slice_in_dim(all_shares, mine_e * local_count, local_count, 1)
+    pieces = []
+    for which in range(local_count):
+        gate_sums = jnp.dot(spread, expert_gate[which], preferred_element_type=jnp.float32)
+        upward = jnp.dot(spread, expert_up[which], preferred_element_type=jnp.float32)
+        value = jax.nn.silu(gate_sums) * upward * own_shares[:, which : which + 1]
+        pieces.append(value.astype(jnp.bfloat16))
+    mixed = jnp.dot(
+        jnp.concatenate(pieces, axis=1),
+        expert_down.reshape(local_count * hidden_part, full_width),
+        preferred_element_type=jnp.float32,
+    ).astype(jnp.bfloat16)
+    columns = jnp.stack([mixed[:, b * part : (b + 1) * part] for b in range(size)])
+    columns = columns.reshape(size, size, rows, part)
+    leaving = []
+    for d in range(size):
+        block_d = pick(columns, mine_t ^ d)
+        leaving.append(jnp.concatenate([block_d[j ^ d] for j in range(size)]))
+    own_columns = traded(leaving, "tensor").reshape(size, rows, part)
+    mixed_here = traded([pick(own_columns, d ^ across) for d in range(size)], "expert")
+    final = (middle.astype(jnp.float32) + mixed_here).astype(jnp.bfloat16)
+    return middle, final
+
+
+def square_body(
+    activations, expert_ids, route_weights, gain_dense, gain_expert, *weights
+):
+    segment_index = lax.axis_index("segment")
+    block = activations[0]
+    ids = pick(expert_ids, segment_index)
+    route = pick(route_weights, segment_index)
+    middle, final = stream(block, ids, route, (gain_dense, gain_expert), weights)
+    other = swap(jnp.where(segment_index == 0, final, middle), "segment", 1)
+    own = jnp.where(segment_index == 0, middle, final)
+    sections = jnp.where(segment_index == 0, jnp.stack([own, other]), jnp.stack([other, own]))
+    return sections[None]
+
+
+def body(activations, expert_ids, *rest):
+    size = lax.axis_size("tensor")
+    groups = lax.axis_size("expert")
+    segments = lax.axis_size("segment")
+    expert_total = rest[4 + 2].shape[0] * groups
+    crowded = 2 * expert_ids.shape[2] >= expert_total
+    if size == groups and size & (size - 1) == 0 and segments == 2 and crowded:
+        return square_body(activations, expert_ids, *rest)
+    return general_body(activations, expert_ids, *rest)
+
+
 def solution(mesh):
     placed = (
         P("segment", "expert", "tensor"),

time: 709 us -> 156 us (0.22)
  waiting for transfers between devices: 531 us -> 77.9 us
  blocking collectives: 58.7 us -> 0 us
  starting transfers between devices: 9.73 us -> 52.9 us
  local copies, waits for them, and re-layouts: 48.6 us -> 10.7 us
  matrix products: 41.3 us -> 8.46 us
  between operations: 13.9 us -> 0.38 us
    all_gather x5 -> x0, waiting for transfers between devices: 439 us -> none  [the longest x1 141 us: dense_folded(): lax.all_gather(dense_up, 'expert', axis=0, tiled=True)]
    unnamed x11 -> x0, waiting for transfers between devices: 77.2 us -> none
    ppermute x1 -> x27, waiting for transfers between devices: 1.25 us -> 77.9 us  [the longest x25 77.9 us: swap(): return lax.ppermute(block, axis, [(i, i ^ distance) for i in devices])]
    ppermute x1 -> x27, starting transfers between devices: 0.07 us -> 52.9 us  [the longest x25 50.6 us: swap(): return lax.ppermute(block, axis, [(i, i ^ distance) for i in devices])]
    all_to_all x2 -> x0, blocking collectives: 38.8 us -> none  [expert_block(): lax.all_to_all(outgoing, 'expert', split_axis=1, concat_axis=1, tiled=True)]
    dot_general x6 -> x8, matrix products: 41.3 us -> 8.46 us  [the longest x2 3.23 us: stream(): jnp.dot(spread, expert_gate[which], preferred_element_type=jnp.float32)]
    unnamed x28 -> x24, local copies, waits for them, and re-layouts: 25.6 us -> 6 us
    all_to_all x2 -> x0, waiting for transfers between devices: 13.9 us -> none  [expert_block(): lax.all_to_all(summed.reshape(local_count, groups, capacity, quarter), 'e...]
  transfers between devices with their start and end apart: 11 -> 27, of which waited for: 10 -> 19; matrix products, arithmetic and copies ran while one was open for 10% -> 2% of each run, Pallas kernels for 0% -> 0%
where the time goes in v1:
time: 156 us; the launch traced here: 155 us
  waiting for transfers between devices  77.9 us (50%)
  starting transfers between devices  52.9 us (34%)
  local copies, waits for them, and re-layouts  10.7 us (7%)
  matrix products  8.46 us (5%)
  other arithmetic  4.72 us (3%)
    ppermute x25, waiting for transfers between devices, swap(): return lax.ppermute(block, axis, [(i, i ^ distance) for i in devices])  77.9 us
    ppermute x25, starting transfers between devices, swap(): return lax.ppermute(block, axis, [(i, i ^ distance) for i in devices])  50.6 us
    unnamed x24, local copies, waits for them, and re-layouts  6 us
    dot_general x2, matrix products, stream(): jnp.dot(spread, expert_gate[which], preferred_element_type=jnp.float32)  3.23 us
  transfers between devices with their start and end apart: 27, of which 19 were waited for; matrix products, arithmetic and copies ran while one was open for 2% of the time, Pallas kernels for 0%

profile of v1, /device:TPU:0, one launch (start us, length us, event | category | flops | bytes accessed | tf_op | source)
XLA Modules:
  0.0 155.1 jit_solution(1421072483614787170)
XLA Ops:
  0.0 1.7 %collective-permute-start = (bf16[64,640]{1,0:T(8,128)(2,1)}, bf16[64,640]{1,0:T(8,128)(2,1)S(1)}, u32[]{:S(2)}, u32[]{:S(2)}) collective-permute-start(bf16[64,640]{1,0:T(8,128)(2,1)} %bitcast.161), channel_id=1, source_target_pairs={{0,0},{1,4},{2,8},{3,12},{4,1},{5,5},{6,9},{7,13},{8,2},{9,6},{10,... | collective-permute-start | bytes 245768 | tf_op jit(solution)/shard_map/ppermute | solution.py:173
  2.4 11.5 %collective-permute-start.1 = (bf16[64,640]{1,0:T(8,128)(2,1)S(1)}, bf16[64,640]{1,0:T(8,128)(2,1)S(1)}, u32[]{:S(2)}, u32[]{:S(2)}) collective-permute-start(bf16[64,640]{1,0:T(8,128)(2,1)S(1)} %collective-permute-done), channel_id=1, source_target_pairs={{0,1},{1,0},{2,3},{3,2},{4,5},{5,4},{6,7},{7,6},{8,9},{9,8},{10,11... | collective-permute-start | bytes 245768 | tf_op jit(solution)/shard_map/ppermute | solution.py:167
  18.4 1.7 %collective-permute-done.3 = bf16[64,640]{1,0:T(8,128)(2,1)S(1)} collective-permute-done((bf16[64,640]{1,0:T(8,128)(2,1)S(1)}, bf16[64,640]{1,0:T(8,128)(2,1)S(1)}, u32[]{:S(2)}, u32[]{:S(2)}) %collective-permute-start.3) | collective-permute-done | bytes 81952 | tf_op jit(solution)/shard_map/ppermute | solution.py:167
  26.6 3.3 %collective-permute-start.5 = (bf16[64,3200]{1,0:T(8,128)(2,1)}, bf16[64,3200]{1,0:T(8,128)(2,1)S(1)}, u32[]{:S(2)}, u32[]{:S(2)}) collective-permute-start(bf16[64,3200]{1,0:T(8,128)(2,1)} %get-tuple-element.9), channel_id=1, source_target_pairs={{0,8},{4,12},{8,0},{12,4},{1,9},{5,13},{9,1},{13,5},{2,10},{6,14},... | collective-permute-start | bytes 1228808 | tf_op jit(solution)/shard_map/ppermute | solution.py:167
  31.1 11.3 %collective-permute-done.4 = bf16[64,3200]{1,0:T(8,128)(2,1)S(1)} collective-permute-done((bf16[64,3200]{1,0:T(8,128)(2,1)}, bf16[64,3200]{1,0:T(8,128)(2,1)S(1)}, u32[]{:S(2)}, u32[]{:S(2)}) %collective-permute-start.4) | collective-permute-done | bytes 409632 | tf_op jit(solution)/shard_map/ppermute | solution.py:167
  42.4 15.6 %collective-permute-done.5 = bf16[64,3200]{1,0:T(8,128)(2,1)S(1)} collective-permute-done((bf16[64,3200]{1,0:T(8,128)(2,1)}, bf16[64,3200]{1,0:T(8,128)(2,1)S(1)}, u32[]{:S(2)}, u32[]{:S(2)}) %collective-permute-start.5) | collective-permute-done | bytes 409632 | tf_op jit(solution)/shard_map/ppermute | solution.py:167
  59.8 5.4 %collective-permute-start.7 = (bf16[64,1664]{1,0:T(8,128)(2,1)S(1)}, bf16[64,1664]{1,0:T(8,128)(2,1)S(1)}, u32[]{:S(2)}, u32[]{:S(2)}) collective-permute-start(bf16[64,1664]{1,0:T(8,128)(2,1)S(1)} %get-tuple-element.45), channel_id=1, source_target_pairs={{0,4},{4,0},{8,12},{12,8},{1,5},{5,1},{9,13},{13,9},{2,6},{6,2},{1... | collective-permute-start | bytes 638984 | tf_op jit(solution)/shard_map/ppermute | solution.py:167
  65.2 1.8 %collective-permute-start.8 = (bf16[64,1664]{1,0:T(8,128)(2,1)S(1)}, bf16[64,1664]{1,0:T(8,128)(2,1)S(1)}, u32[]{:S(2)}, u32[]{:S(2)}) collective-permute-start(bf16[64,1664]{1,0:T(8,128)(2,1)S(1)} %get-tuple-element.45), channel_id=1, source_target_pairs={{0,8},{4,12},{8,0},{12,4},{1,9},{5,13},{9,1},{13,5},{2,10},{6,14},... | collective-permute-start | bytes 638984 | tf_op jit(solution)/shard_map/ppermute | solution.py:167
  67.0 1.4 collective-permute-start.9
  68.4 2.4 %collective-permute-done.7 = bf16[64,1664]{1,0:T(8,128)(2,1)S(1)} collective-permute-done((bf16[64,1664]{1,0:T(8,128)(2,1)S(1)}, bf16[64,1664]{1,0:T(8,128)(2,1)S(1)}, u32[]{:S(2)}, u32[]{:S(2)}) %collective-permute-start.7) | collective-permute-done | bytes 213024 | tf_op jit(solution)/shard_map/ppermute | solution.py:167
  70.8 10.1 %collective-permute-done.8 = bf16[64,1664]{1,0:T(8,128)(2,1)S(1)} collective-permute-done((bf16[64,1664]{1,0:T(8,128)(2,1)S(1)}, bf16[64,1664]{1,0:T(8,128)(2,1)S(1)}, u32[]{:S(2)}, u32[]{:S(2)}) %collective-permute-start.8) | collective-permute-done | bytes 213024 | tf_op jit(solution)/shard_map/ppermute | solution.py:167
  81.1 1.3 copy-done.9
  83.3 1.3 collective-permute-start.10
  84.6 3.9 %collective-permute-start.11 = (bf16[64,640]{1,0:T(8,128)(2,1)S(1)}, bf16[64,640]{1,0:T(8,128)(2,1)S(1)}, u32[]{:S(2)}, u32[]{:S(2)}) collective-permute-start(bf16[64,640]{1,0:T(8,128)(2,1)S(1)} %get-tuple-element.39), channel_id=1, source_target_pairs={{0,2},{1,3},{2,0},{3,1},{4,6},{5,7},{6,4},{7,5},{8,10},{9,11},{10,... | collective-permute-start | bytes 245768 | tf_op jit(solution)/shard_map/ppermute | solution.py:167
  88.7 2.3 %collective-permute-done.11 = bf16[64,640]{1,0:T(8,128)(2,1)S(1)} collective-permute-done((bf16[64,640]{1,0:T(8,128)(2,1)S(1)}, bf16[64,640]{1,0:T(8,128)(2,1)S(1)}, u32[]{:S(2)}, u32[]{:S(2)}) %collective-permute-start.11) | collective-permute-done | bytes 81952 | tf_op jit(solution)/shard_map/ppermute | solution.py:167
  91.0 2.9 %collective-permute-done.12 = bf16[64,640]{1,0:T(8,128)(2,1)S(1)} collective-permute-done((bf16[64,640]{1,0:T(8,128)(2,1)S(1)}, bf16[64,640]{1,0:T(8,128)(2,1)S(1)}, u32[]{:S(2)}, u32[]{:S(2)}) %collective-permute-start.12) | collective-permute-done | bytes 81952 | tf_op jit(solution)/shard_map/ppermute | solution.py:167
  94.0 3.0 %collective-permute-start.14 = (bf16[64,640]{1,0:T(8,128)(2,1)S(1)}, bf16[64,640]{1,0:T(8,128)(2,1)S(1)}, u32[]{:S(2)}, u32[]{:S(2)}) collective-permute-start(bf16[64,640]{1,0:T(8,128)(2,1)S(1)} %fusion.31), channel_id=1, source_target_pairs={{0,4},{4,0},{8,12},{12,8},{1,5},{5,1},{9,13},{13,9},{2,6},{6,2},{1... | collective-permute-start | bytes 245768 | tf_op jit(solution)/shard_map/ppermute | solution.py:167
  97.0 2.0 %collective-permute-start.15 = (bf16[64,640]{1,0:T(8,128)(2,1)S(1)}, bf16[64,640]{1,0:T(8,128)(2,1)S(1)}, u32[]{:S(2)}, u32[]{:S(2)}) collective-permute-start(bf16[64,640]{1,0:T(8,128)(2,1)S(1)} %fusion.31), channel_id=1, source_target_pairs={{0,8},{4,12},{8,0},{12,4},{1,9},{5,13},{9,1},{13,5},{2,10},{6,14},... | collective-permute-start | bytes 245768 | tf_op jit(solution)/shard_map/ppermute | solution.py:167
  99.0 1.4 collective-permute-start.16
  100.7 2.0 %collective-permute-done.15 = bf16[64,640]{1,0:T(8,128)(2,1)S(1)} collective-permute-done((bf16[64,640]{1,0:T(8,128)(2,1)S(1)}, bf16[64,640]{1,0:T(8,128)(2,1)S(1)}, u32[]{:S(2)}, u32[]{:S(2)}) %collective-permute-start.15) | collective-permute-done | bytes 81952 | tf_op jit(solution)/shard_map/ppermute | solution.py:167
  102.6 2.7 %collective-permute-done.16 = bf16[64,640]{1,0:T(8,128)(2,1)S(1)} collective-permute-done((bf16[64,640]{1,0:T(8,128)(2,1)S(1)}, bf16[64,640]{1,0:T(8,128)(2,1)S(1)}, u32[]{:S(2)}, u32[]{:S(2)}) %collective-permute-start.16) | collective-permute-done | bytes 81952 | tf_op jit(solution)/shard_map/ppermute | solution.py:167
  106.4 2.9 %collective-permute-start.19 = (bf16[64,2560]{1,0:T(8,128)(2,1)S(1)}, bf16[64,2560]{1,0:T(8,128)(2,1)S(1)}, u32[]{:S(2)}, u32[]{:S(2)}) collective-permute-start(bf16[64,2560]{1,0:T(8,128)(2,1)S(1)} %fusion.18), channel_id=1, source_target_pairs={{0,3},{1,2},{2,1},{3,0},{4,7},{5,6},{6,5},{7,4},{8,11},{9,10},{10,... | collective-permute-start | bytes 983048 | tf_op jit(solution)/shard_map/ppermute | solution.py:167
  109.3 5.4 %collective-permute-done.17 = bf16[64,2560]{1,0:T(8,128)(2,1)S(1)} collective-permute-done((bf16[64,2560]{1,0:T(8,128)(2,1)S(1)}, bf16[64,2560]{1,0:T(8,128)(2,1)S(1)}, u32[]{:S(2)}, u32[]{:S(2)}) %collective-permute-start.17) | collective-permute-done | bytes 327712 | tf_op jit(solution)/shard_map/ppermute | solution.py:167
  114.7 3.6 %collective-permute-done.18 = bf16[64,2560]{1,0:T(8,128)(2,1)S(1)} collective-permute-done((bf16[64,2560]{1,0:T(8,128)(2,1)S(1)}, bf16[64,2560]{1,0:T(8,128)(2,1)S(1)}, u32[]{:S(2)}, u32[]{:S(2)}) %collective-permute-start.18) | collective-permute-done | bytes 327712 | tf_op jit(solution)/shard_map/ppermute | solution.py:167
  118.3 2.4 %fusion.7 = f32[256,384]{1,0:T(8,128)S(1)} fusion(bf16[2,2560,384]{2,1,0:T(8,128)(2,1)} %param.19, bf16[64,2560]{1,0:T(8,128)(2,1)S(1)} %collective-permute-done.19, bf16[64,2560]{1,0:T(8,128)(2,1)S(1)} %collective-permute-done.18, bf16[64,2560]{1,0:T(8,128)(2,1)S(1)} %collective-permute-done.17, bf16[64,2560]{1,0:T(8,128)(2,1)S(1)} %fusion.18), kind=kOutput, calls=%fused_computation.11 | convolution fusion | flops 508559360 | bytes 3670016 | tf_op jit(solution)/shard_map/dot_general | solution.py:267
  127.6 1.7 %collective-permute-start.20 = (bf16[256,640]{1,0:T(8,128)(2,1)S(1)}, bf16[256,640]{1,0:T(8,128)(2,1)S(1)}, u32[]{:S(2)}, u32[]{:S(2)}) collective-permute-start(bf16[256,640]{1,0:T(8,128)(2,1)S(1)} %pad_maximum_fusion.7), channel_id=1, source_target_pairs={{0,1},{1,0},{2,3},{3,2},{4,5},{5,4},{6,7},{7,6},{8,9},{9,8},{10,11... | collective-permute-start | bytes 983048 | tf_op jit(solution)/shard_map/ppermute | solution.py:167
  129.7 1.6 %collective-permute-start.22 = (bf16[256,640]{1,0:T(8,128)(2,1)S(1)}, bf16[256,640]{1,0:T(8,128)(2,1)S(1)}, u32[]{:S(2)}, u32[]{:S(2)}) collective-permute-start(bf16[256,640]{1,0:T(8,128)(2,1)S(1)} %pad_maximum_fusion.9), channel_id=1, source_target_pairs={{0,3},{1,2},{2,1},{3,0},{4,7},{5,6},{6,5},{7,4},{8,11},{9,10},{10,... | collective-permute-start | bytes 983048 | tf_op jit(solution)/shard_map/ppermute | solution.py:167
  132.0 3.4 %collective-permute-done.20 = bf16[256,640]{1,0:T(8,128)(2,1)S(1)} collective-permute-done((bf16[256,640]{1,0:T(8,128)(2,1)S(1)}, bf16[256,640]{1,0:T(8,128)(2,1)S(1)}, u32[]{:S(2)}, u32[]{:S(2)}) %collective-permute-start.20) | collective-permute-done | bytes 327712 | tf_op jit(solution)/shard_map/ppermute | solution.py:167
  135.4 4.8 %collective-permute-done.21 = bf16[256,640]{1,0:T(8,128)(2,1)S(1)} collective-permute-done((bf16[256,640]{1,0:T(8,128)(2,1)S(1)}, bf16[256,640]{1,0:T(8,128)(2,1)S(1)}, u32[]{:S(2)}, u32[]{:S(2)}) %collective-permute-start.21) | collective-permute-done | bytes 327712 | tf_op jit(solution)/shard_map/ppermute | solution.py:167
  142.3 4.4 %collective-permute-start.24 = (bf16[64,640]{1,0:T(8,128)(2,1)S(1)}, bf16[64,640]{1,0:T(8,128)(2,1)S(1)}, u32[]{:S(2)}, u32[]{:S(2)}) collective-permute-start(bf16[64,640]{1,0:T(8,128)(2,1)S(1)} %get-tuple-element.32), channel_id=1, source_target_pairs={{0,8},{4,12},{8,0},{12,4},{1,9},{5,13},{9,1},{13,5},{2,10},{6,14},... | collective-permute-start | bytes 245768 | tf_op jit(solution)/shard_map/ppermute | solution.py:167
  146.7 3.3 %collective-permute-done.24 = bf16[64,640]{1,0:T(8,128)(2,1)S(1)} collective-permute-done((bf16[64,640]{1,0:T(8,128)(2,1)S(1)}, bf16[64,640]{1,0:T(8,128)(2,1)S(1)}, u32[]{:S(2)}, u32[]{:S(2)}) %collective-permute-start.24) | collective-permute-done | bytes 81952 | tf_op jit(solution)/shard_map/ppermute | solution.py:167
  150.0 2.9 %collective-permute-done.25 = bf16[64,640]{1,0:T(8,128)(2,1)S(1)} collective-permute-done((bf16[64,640]{1,0:T(8,128)(2,1)S(1)}, bf16[64,640]{1,0:T(8,128)(2,1)S(1)}, u32[]{:S(2)}, u32[]{:S(2)}) %collective-permute-start.25) | collective-permute-done | bytes 81952 | tf_op jit(solution)/shard_map/ppermute | solution.py:167
  (100 shorter events, 29.2 us)
Async XLA Ops:
  0.0 20.4 %copy-start = (bf16[640,1536]{1,0:T(8,128)(2,1)S(1)}, bf16[640,1536]{1,0:T(8,128)(2,1)}, u32[]{:S(2)}) copy-start(bf16[640,1536]{1,0:T(8,128)(2,1)} %param.16) | copy-start | bytes 5898244
  0.0 2.4 %collective-permute-start = (bf16[64,640]{1,0:T(8,128)(2,1)}, bf16[64,640]{1,0:T(8,128)(2,1)S(1)}, u32[]{:S(2)}, u32[]{:S(2)}) collective-permute-start(bf16[64,640]{1,0:T(8,128)(2,1)} %bitcast.161), channel_id=1, source_target_pairs={{0,0},{1,4},{2,8},{3,12},{4,1},{5,5},{6,9},{7,13},{8,2},{9,6},{10,... | collective-permute-start | bytes 245768 | tf_op jit(solution)/shard_map/ppermute | solution.py:173
  2.4 17.8 %copy-start.2 = (bf16[64,640]{1,0:T(8,128)(2,1)}, bf16[64,640]{1,0:T(8,128)(2,1)S(1)}, u32[]{:S(2)}) copy-start(bf16[64,640]{1,0:T(8,128)(2,1)S(1)} %collective-permute-done) | copy-start | bytes 245764
  2.4 14.7 %collective-permute-start.1 = (bf16[64,640]{1,0:T(8,128)(2,1)S(1)}, bf16[64,640]{1,0:T(8,128)(2,1)S(1)}, u32[]{:S(2)}, u32[]{:S(2)}) collective-permute-start(bf16[64,640]{1,0:T(8,128)(2,1)S(1)} %collective-permute-done), channel_id=1, source_target_pairs={{0,1},{1,0},{2,3},{3,2},{4,5},{5,4},{6,7},{7,6},{8,9},{9,8},{10,11... | collective-permute-start | bytes 245768 | tf_op jit(solution)/shard_map/ppermute | solution.py:167
  13.9 4.5 %collective-permute-start.2 = (bf16[64,640]{1,0:T(8,128)(2,1)S(1)}, bf16[64,640]{1,0:T(8,128)(2,1)S(1)}, u32[]{:S(2)}, u32[]{:S(2)}) collective-permute-start(bf16[64,640]{1,0:T(8,128)(2,1)S(1)} %collective-permute-done), channel_id=1, source_target_pairs={{0,2},{1,3},{2,0},{3,1},{4,6},{5,7},{6,4},{7,5},{8,10},{9,11},{10,... | collective-permute-start | bytes 245768 | tf_op jit(solution)/shard_map/ppermute | solution.py:167
  14.8 5.3 %collective-permute-start.3 = (bf16[64,640]{1,0:T(8,128)(2,1)S(1)}, bf16[64,640]{1,0:T(8,128)(2,1)S(1)}, u32[]{:S(2)}, u32[]{:S(2)}) collective-permute-start(bf16[64,640]{1,0:T(8,128)(2,1)S(1)} %collective-permute-done), channel_id=1, source_target_pairs={{0,3},{1,2},{2,1},{3,0},{4,7},{5,6},{6,5},{7,4},{8,11},{9,10},{10,... | collective-permute-start | bytes 245768 | tf_op jit(solution)/shard_map/ppermute | solution.py:167
  26.6 15.8 %collective-permute-start.4 = (bf16[64,3200]{1,0:T(8,128)(2,1)}, bf16[64,3200]{1,0:T(8,128)(2,1)S(1)}, u32[]{:S(2)}, u32[]{:S(2)}) collective-permute-start(bf16[64,3200]{1,0:T(8,128)(2,1)} %get-tuple-element.7), channel_id=1, source_target_pairs={{0,4},{4,0},{8,12},{12,8},{1,5},{5,1},{9,13},{13,9},{2,6},{6,2},{1... | collective-permute-start | bytes 1228808 | tf_op jit(solution)/shard_map/ppermute | solution.py:167
  26.6 31.4 %collective-permute-start.5 = (bf16[64,3200]{1,0:T(8,128)(2,1)}, bf16[64,3200]{1,0:T(8,128)(2,1)S(1)}, u32[]{:S(2)}, u32[]{:S(2)}) collective-permute-start(bf16[64,3200]{1,0:T(8,128)(2,1)} %get-tuple-element.9), channel_id=1, source_target_pairs={{0,8},{4,12},{8,0},{12,4},{1,9},{5,13},{9,1},{13,5},{2,10},{6,14},... | collective-permute-start | bytes 1228808 | tf_op jit(solution)/shard_map/ppermute | solution.py:167
  29.9 28.1 %collective-permute-start.6 = (bf16[64,3200]{1,0:T(8,128)(2,1)S(1)}, bf16[64,3200]{1,0:T(8,128)(2,1)}, u32[]{:S(2)}, u32[]{:S(2)}) collective-permute-start(bf16[64,3200]{1,0:T(8,128)(2,1)S(1)} %get-tuple-element.8), channel_id=1, source_target_pairs={{0,12},{4,8},{8,4},{12,0},{1,13},{5,9},{9,5},{13,1},{2,14},{6,10},... | collective-permute-start | bytes 1228808 | tf_op jit(solution)/shard_map/ppermute | solution.py:167
  59.8 11.0 %collective-permute-start.7 = (bf16[64,1664]{1,0:T(8,128)(2,1)S(1)}, bf16[64,1664]{1,0:T(8,128)(2,1)S(1)}, u32[]{:S(2)}, u32[]{:S(2)}) collective-permute-start(bf16[64,1664]{1,0:T(8,128)(2,1)S(1)} %get-tuple-element.45), channel_id=1, source_target_pairs={{0,4},{4,0},{8,12},{12,8},{1,5},{5,1},{9,13},{13,9},{2,6},{6,2},{1... | collective-permute-start | bytes 638984 | tf_op jit(solution)/shard_map/ppermute | solution.py:167
  65.2 15.7 %collective-permute-start.8 = (bf16[64,1664]{1,0:T(8,128)(2,1)S(1)}, bf16[64,1664]{1,0:T(8,128)(2,1)S(1)}, u32[]{:S(2)}, u32[]{:S(2)}) collective-permute-start(bf16[64,1664]{1,0:T(8,128)(2,1)S(1)} %get-tuple-element.45), channel_id=1, source_target_pairs={{0,8},{4,12},{8,0},{12,4},{1,9},{5,13},{9,1},{13,5},{2,10},{6,14},... | collective-permute-start | bytes 638984 | tf_op jit(solution)/shard_map/ppermute | solution.py:167
  67.0 13.9 %collective-permute-start.9 = (bf16[64,1664]{1,0:T(8,128)(2,1)S(1)}, bf16[64,1664]{1,0:T(8,128)(2,1)S(1)}, u32[]{:S(2)}, u32[]{:S(2)}) collective-permute-start(bf16[64,1664]{1,0:T(8,128)(2,1)S(1)} %get-tuple-element.45), channel_id=1, source_target_pairs={{0,12},{4,8},{8,4},{12,0},{1,13},{5,9},{9,5},{13,1},{2,14},{6,10},... | collective-permute-start | bytes 638984 | tf_op jit(solution)/shard_map/ppermute | solution.py:167
  82.5 11.5 %copy-start.3 = (bf16[64,640]{1,0:T(8,128)(2,1)S(1)}, bf16[64,640]{1,0:T(8,128)(2,1)}, u32[]{:S(2)}) copy-start(bf16[64,640]{1,0:T(8,128)(2,1)} %copy-done.2) | copy-start | bytes 245764
  83.3 22.3 %copy-start.4 = (f32[2560]{0:T(1024)S(1)}, f32[2560]{0:T(1024)}, u32[]{:S(2)}) copy-start(f32[2560]{0:T(1024)} %param.15) | copy-start | bytes 30724
  83.3 5.4 %collective-permute-start.10 = (bf16[64,640]{1,0:T(8,128)(2,1)S(1)}, bf16[64,640]{1,0:T(8,128)(2,1)S(1)}, u32[]{:S(2)}, u32[]{:S(2)}) collective-permute-start(bf16[64,640]{1,0:T(8,128)(2,1)S(1)} %get-tuple-element.37), channel_id=1, source_target_pairs={{0,1},{1,0},{2,3},{3,2},{4,5},{5,4},{6,7},{7,6},{8,9},{9,8},{10,11... | collective-permute-start | bytes 245768 | tf_op jit(solution)/shard_map/ppermute | solution.py:167
  84.6 6.4 %collective-permute-start.11 = (bf16[64,640]{1,0:T(8,128)(2,1)S(1)}, bf16[64,640]{1,0:T(8,128)(2,1)S(1)}, u32[]{:S(2)}, u32[]{:S(2)}) collective-permute-start(bf16[64,640]{1,0:T(8,128)(2,1)S(1)} %get-tuple-element.39), channel_id=1, source_target_pairs={{0,2},{1,3},{2,0},{3,1},{4,6},{5,7},{6,4},{7,5},{8,10},{9,11},{10,... | collective-permute-start | bytes 245768 | tf_op jit(solution)/shard_map/ppermute | solution.py:167
  88.6 5.3 %collective-permute-start.12 = (bf16[64,640]{1,0:T(8,128)(2,1)S(1)}, bf16[64,640]{1,0:T(8,128)(2,1)S(1)}, u32[]{:S(2)}, u32[]{:S(2)}) collective-permute-start(bf16[64,640]{1,0:T(8,128)(2,1)S(1)} %get-tuple-element.38), channel_id=1, source_target_pairs={{0,3},{1,2},{2,1},{3,0},{4,7},{5,6},{6,5},{7,4},{8,11},{9,10},{10,... | collective-permute-start | bytes 245768 | tf_op jit(solution)/shard_map/ppermute | solution.py:167
  94.0 6.7 %collective-permute-start.14 = (bf16[64,640]{1,0:T(8,128)(2,1)S(1)}, bf16[64,640]{1,0:T(8,128)(2,1)S(1)}, u32[]{:S(2)}, u32[]{:S(2)}) collective-permute-start(bf16[64,640]{1,0:T(8,128)(2,1)S(1)} %fusion.31), channel_id=1, source_target_pairs={{0,4},{4,0},{8,12},{12,8},{1,5},{5,1},{9,13},{13,9},{2,6},{6,2},{1... | collective-permute-start | bytes 245768 | tf_op jit(solution)/shard_map/ppermute | solution.py:167
  97.0 5.7 %collective-permute-start.15 = (bf16[64,640]{1,0:T(8,128)(2,1)S(1)}, bf16[64,640]{1,0:T(8,128)(2,1)S(1)}, u32[]{:S(2)}, u32[]{:S(2)}) collective-permute-start(bf16[64,640]{1,0:T(8,128)(2,1)S(1)} %fusion.31), channel_id=1, source_target_pairs={{0,8},{4,12},{8,0},{12,4},{1,9},{5,13},{9,1},{13,5},{2,10},{6,14},... | collective-permute-start | bytes 245768 | tf_op jit(solution)/shard_map/ppermute | solution.py:167
  99.0 6.3 %collective-permute-start.16 = (bf16[64,640]{1,0:T(8,128)(2,1)S(1)}, bf16[64,640]{1,0:T(8,128)(2,1)S(1)}, u32[]{:S(2)}, u32[]{:S(2)}) collective-permute-start(bf16[64,640]{1,0:T(8,128)(2,1)S(1)} %fusion.31), channel_id=1, source_target_pairs={{0,12},{4,8},{8,4},{12,0},{1,13},{5,9},{9,5},{13,1},{2,14},{6,10},... | collective-permute-start | bytes 245768 | tf_op jit(solution)/shard_map/ppermute | solution.py:167
  105.8 9.0 %collective-permute-start.17 = (bf16[64,2560]{1,0:T(8,128)(2,1)S(1)}, bf16[64,2560]{1,0:T(8,128)(2,1)S(1)}, u32[]{:S(2)}, u32[]{:S(2)}) collective-permute-start(bf16[64,2560]{1,0:T(8,128)(2,1)S(1)} %fusion.18), channel_id=1, source_target_pairs={{0,1},{1,0},{2,3},{3,2},{4,5},{5,4},{6,7},{7,6},{8,9},{9,8},{10,11... | collective-permute-start | bytes 983048 | tf_op jit(solution)/shard_map/ppermute | solution.py:167
  105.9 12.4 %collective-permute-start.18 = (bf16[64,2560]{1,0:T(8,128)(2,1)S(1)}, bf16[64,2560]{1,0:T(8,128)(2,1)S(1)}, u32[]{:S(2)}, u32[]{:S(2)}) collective-permute-start(bf16[64,2560]{1,0:T(8,128)(2,1)S(1)} %fusion.18), channel_id=1, source_target_pairs={{0,2},{1,3},{2,0},{3,1},{4,6},{5,7},{6,4},{7,5},{8,10},{9,11},{10,... | collective-permute-start | bytes 983048 | tf_op jit(solution)/shard_map/ppermute | solution.py:167
  106.4 11.9 %collective-permute-start.19 = (bf16[64,2560]{1,0:T(8,128)(2,1)S(1)}, bf16[64,2560]{1,0:T(8,128)(2,1)S(1)}, u32[]{:S(2)}, u32[]{:S(2)}) collective-permute-start(bf16[64,2560]{1,0:T(8,128)(2,1)S(1)} %fusion.18), channel_id=1, source_target_pairs={{0,3},{1,2},{2,1},{3,0},{4,7},{5,6},{6,5},{7,4},{8,11},{9,10},{10,... | collective-permute-start | bytes 983048 | tf_op jit(solution)/shard_map/ppermute | solution.py:167
  109.3 11.4 %copy-start.5 = (bf16[2,2560,384]{2,1,0:T(8,128)(2,1)S(1)}, bf16[2,2560,384]{2,1,0:T(8,128)(2,1)}, u32[]{:S(2)}) copy-start(bf16[2,2560,384]{2,1,0:T(8,128)(2,1)} %param.19) | copy-start | bytes 11796484
  127.6 7.9 %collective-permute-start.20 = (bf16[256,640]{1,0:T(8,128)(2,1)S(1)}, bf16[256,640]{1,0:T(8,128)(2,1)S(1)}, u32[]{:S(2)}, u32[]{:S(2)}) collective-permute-start(bf16[256,640]{1,0:T(8,128)(2,1)S(1)} %pad_maximum_fusion.7), channel_id=1, source_target_pairs={{0,1},{1,0},{2,3},{3,2},{4,5},{5,4},{6,7},{7,6},{8,9},{9,8},{10,11... | collective-permute-start | bytes 983048 | tf_op jit(solution)/shard_map/ppermute | solution.py:167
  129.4 10.9 %collective-permute-start.21 = (bf16[256,640]{1,0:T(8,128)(2,1)S(1)}, bf16[256,640]{1,0:T(8,128)(2,1)S(1)}, u32[]{:S(2)}, u32[]{:S(2)}) collective-permute-start(bf16[256,640]{1,0:T(8,128)(2,1)S(1)} %pad_maximum_fusion.8), channel_id=1, source_target_pairs={{0,2},{1,3},{2,0},{3,1},{4,6},{5,7},{6,4},{7,5},{8,10},{9,11},{10,... | collective-permute-start | bytes 983048 | tf_op jit(solution)/shard_map/ppermute | solution.py:167
  129.7 11.0 %collective-permute-start.22 = (bf16[256,640]{1,0:T(8,128)(2,1)S(1)}, bf16[256,640]{1,0:T(8,128)(2,1)S(1)}, u32[]{:S(2)}, u32[]{:S(2)}) collective-permute-start(bf16[256,640]{1,0:T(8,128)(2,1)S(1)} %pad_maximum_fusion.9), channel_id=1, source_target_pairs={{0,3},{1,2},{2,1},{3,0},{4,7},{5,6},{6,5},{7,4},{8,11},{9,10},{10,... | collective-permute-start | bytes 983048 | tf_op jit(solution)/shard_map/ppermute | solution.py:167
  131.3 15.4 %collective-permute-start.13 = (bf16[64,640]{1,0:T(8,128)(2,1)S(1)}, bf16[64,640]{1,0:T(8,128)(2,1)S(1)}, u32[]{:S(2)}, u32[]{:S(2)}) collective-permute-start(bf16[64,640]{1,0:T(8,128)(2,1)S(1)} %fusion.31), channel_id=1, source_target_pairs={{0,0},{1,4},{2,8},{3,12},{4,1},{5,5},{6,9},{7,13},{8,2},{9,6},{10,... | collective-permute-start | bytes 245768 | tf_op jit(solution)/shard_map/ppermute | solution.py:173
  141.0 5.7 %collective-permute-start.23 = (bf16[64,640]{1,0:T(8,128)(2,1)S(1)}, bf16[64,640]{1,0:T(8,128)(2,1)S(1)}, u32[]{:S(2)}, u32[]{:S(2)}) collective-permute-start(bf16[64,640]{1,0:T(8,128)(2,1)S(1)} %get-tuple-element.30), channel_id=1, source_target_pairs={{0,4},{4,0},{8,12},{12,8},{1,5},{5,1},{9,13},{13,9},{2,6},{6,2},{1... | collective-permute-start | bytes 245768 | tf_op jit(solution)/shard_map/ppermute | solution.py:167
  142.3 7.7 %collective-permute-start.24 = (bf16[64,640]{1,0:T(8,128)(2,1)S(1)}, bf16[64,640]{1,0:T(8,128)(2,1)S(1)}, u32[]{:S(2)}, u32[]{:S(2)}) collective-permute-start(bf16[64,640]{1,0:T(8,128)(2,1)S(1)} %get-tuple-element.32), channel_id=1, source_target_pairs={{0,8},{4,12},{8,0},{12,4},{1,9},{5,13},{9,1},{13,5},{2,10},{6,14},... | collective-permute-start | bytes 245768 | tf_op jit(solution)/shard_map/ppermute | solution.py:167
  146.7 6.2 %collective-permute-start.25 = (bf16[64,640]{1,0:T(8,128)(2,1)S(1)}, bf16[64,640]{1,0:T(8,128)(2,1)S(1)}, u32[]{:S(2)}, u32[]{:S(2)}) collective-permute-start(bf16[64,640]{1,0:T(8,128)(2,1)S(1)} %get-tuple-element.31), channel_id=1, source_target_pairs={{0,12},{4,8},{8,4},{12,0},{1,13},{5,9},{9,5},{13,1},{2,14},{6,10},... | collective-permute-start | bytes 245768 | tf_op jit(solution)/shard_map/ppermute | solution.py:167
  153.0 1.3 collective-permute-start.26
  (5 other events, 8.5 us)

commit v2 on v0

--- a/solution.py
+++ b/solution.py
@@ -1,7 +1,10 @@
 import jax
 import jax.numpy as jnp
 from jax import lax
+from jax.experimental import pallas as pl
+from jax.experimental.pallas import tpu as pltpu
 from jax.sharding import PartitionSpec as P
+
 
 EPSILON = 1e-06
 
@@ -18,7 +21,7 @@
 
 
 def dense_prepare(micro_block, gain_dense):
-    micro_count, tokens_here, quarter = micro_block.shape
+    micro_count, tokens_here, _ = micro_block.shape
     whole_rows = lax.all_gather(micro_block, "tensor", axis=2, tiled=True)
     full_width = whole_rows.shape[2]
     normed = normalize(whole_rows.astype(jnp.float32), gain_dense).astype(jnp.bfloat16)
@@ -26,7 +29,7 @@
 
 
 def dense_finish(micro_block, partial_value):
-    micro_count, tokens_here, quarter = micro_block.shape
+    micro_count, tokens_here, _ = micro_block.shape
     summed = lax.psum_scatter(
         partial_value.reshape(micro_count, tokens_here, partial_value.shape[1]).astype(
             jnp.bfloat16
@@ -85,7 +88,7 @@
     tokens_here, quarter = middle.shape
     picks = expert_ids_block.shape[1]
     groups = lax.axis_size("expert")
-    local_count, full_width, hidden_part = expert_gate.shape
+    local_count, full_width, _ = expert_gate.shape
     capacity = min(tokens_here, 2 * (tokens_here * picks // (local_count * groups)))
     slots, sources = route_slots(expert_ids_block, local_count, groups, capacity)
     middle_wide = middle.astype(jnp.float32)
@@ -123,7 +126,7 @@
     return (middle_wide + mixed).astype(jnp.bfloat16)
 
 
-def body(
+def general_body(
     activations,
     expert_ids,
     route_weights,
@@ -162,6 +165,247 @@
     return sections[None]
 
 
+def swap(block, axis, distance):
+    devices = range(lax.axis_size(axis))
+    return lax.ppermute(block, axis, [(i, i ^ distance) for i in devices])
+
+
+def transposed(block):
+    size = lax.axis_size("tensor")
+    route = [(a * size + b, b * size + a) for a in range(size) for b in range(size)]
+    return lax.ppermute(block, ("expert", "tensor"), route)
+
+
+def gathered(block, axis):
+    size = lax.axis_size(axis)
+    arrived = {d: swap(block, axis, d) for d in range(size - 1, 0, -1)}
+    return [block] + [arrived[d] for d in range(1, size)]
+
+
+def traded(blocks, axis):
+    size = lax.axis_size(axis)
+    sent = {d: swap(blocks[d].astype(jnp.bfloat16), axis, d) for d in range(size - 1, 0, -1)}
+    total = blocks[0].astype(jnp.float32)
+    for d in range(1, size):
+        total = total + sent[d].astype(jnp.float32)
+    return total
+
+
+def pick(stacked, index):
+    return lax.dynamic_index_in_dim(stacked, index, 0, keepdims=False)
+
+
+LANES = 128
+STEPS = 3
+ON_CHIP = True
+IN_VMEM = pl.BlockSpec(memory_space=pltpu.VMEM)
+IN_SMEM = pl.BlockSpec(memory_space=pltpu.SMEM)
+IN_PLACE = pl.BlockSpec(memory_space=pltpu.HBM)
+
+
+def call(kernel, out_shape, operands, specs, limit, flops, moved, scratch=()):
+    count = len(out_shape)
+    return pl.pallas_call(
+        kernel,
+        out_shape=out_shape,
+        in_specs=specs,
+        out_specs=[IN_VMEM] * count,
+        scratch_shapes=scratch,
+        compiler_params=pltpu.CompilerParams(vmem_limit_bytes=limit),
+        cost_estimate=pl.CostEstimate(flops=flops, bytes_accessed=moved, transcendentals=0),
+    )(*operands)
+
+
+def on_chip(array):
+    return pltpu.with_memory_space_constraint(array, pltpu.VMEM) if ON_CHIP else array
+
+
+def fetch_kernel(*refs):
+    count = len(refs) // 2
+    copies = [
+        pltpu.make_async_copy(refs[i], refs[count + i], refs[-1].at[i]) for i in range(count)
+    ]
+    for copy in copies:
+        copy.start()
+    for copy in copies:
+        copy.wait()
+
+
+def fetched(arrays):
+    return call(
+        fetch_kernel,
+        [pltpu.VMEM(a.shape, a.dtype) if ON_CHIP else jax.ShapeDtypeStruct(a.shape, a.dtype) for a in arrays],
+        arrays,
+        [IN_PLACE] * len(arrays),
+        1 << 20,
+        0,
+        sum(a.size * 2 for a in arrays),
+        [pltpu.SemaphoreType.DMA((len(arrays),))],
+    )
+
+
+def dense_kernel(across_ref, *refs):
+    size = lax.axis_size("tensor")
+    blocks, (gain_ref, *weights), outs = refs[:size], refs[size : size + 3], refs[size + 3 :]
+    hidden = weights[0].shape[1]
+    step = hidden // STEPS
+    across = across_ref[0]
+    gain = gain_ref[...]
+    rows = blocks[0].shape[0]
+    scaled = []
+    for d in range(size):
+        block = blocks[d][...]
+        for other in range(1, size):
+            block = jnp.where(across == other, blocks[d ^ other][...], block)
+        scaled.append((block.astype(jnp.float32) * gain).astype(jnp.bfloat16))
+    tokens = jnp.concatenate(scaled)
+    for which, weight_ref in enumerate(weights):
+        for first in range(0, hidden, step):
+            sums = jnp.dot(
+                tokens, weight_ref[:, first : first + step], preferred_element_type=jnp.float32
+            ).astype(jnp.bfloat16)
+            for d in range(size):
+                outs[which * size + d][:, first : first + step] = sums[d * rows : (d + 1) * rows]
+
+
+def expert_kernel(own_ref, *refs):
+    size = lax.axis_size("tensor")
+    blocks, (share_ref, gate_ref, up_ref, down_ref) = refs[:size], refs[size : size + 4]
+    outs = refs[size + 4 :]
+    local_count, _, _ = gate_ref.shape
+    rows, full_width = blocks[0].shape
+    part = full_width // size
+    own = own_ref[0]
+    spread = jnp.concatenate([block[...] for block in blocks])
+    pieces = []
+    for which in range(local_count):
+        gate = jnp.dot(spread, gate_ref[which], preferred_element_type=jnp.float32)
+        up = jnp.dot(spread, up_ref[which], preferred_element_type=jnp.float32)
+        value = gate / (1.0 + jnp.exp(-gate)) * up * share_ref[:, which : which + 1]
+        pieces.append(value.astype(jnp.bfloat16))
+    for d in range(size):
+        column = pl.multiple_of((own ^ d) * part, LANES)
+        mixed = None
+        for which in range(local_count):
+            term = jnp.dot(
+                pieces[which],
+                down_ref[which, :, pl.ds(column, part)],
+                preferred_element_type=jnp.float32,
+            )
+            mixed = term if mixed is None else mixed + term
+        mixed = mixed.astype(jnp.bfloat16)
+        for j in range(size):
+            outs[d][j * rows : (j + 1) * rows] = mixed[(j ^ d) * rows : ((j ^ d) + 1) * rows]
+
+
+def square_body(activations, expert_ids, route_weights, gain_dense, gain_expert, *weights):
+    dense_gate, dense_up, dense_down, expert_gate, expert_up, expert_down = weights
+    segment_index = lax.axis_index("segment")
+    mine_e, mine_t = lax.axis_index("expert"), lax.axis_index("tensor")
+    across = mine_e ^ mine_t
+    size = lax.axis_size("tensor")
+    block = activations[0]
+    rows, part = block.shape
+    full_width = part * size
+    hidden = dense_gate.shape[1]
+    local_count, _, hidden_part = expert_gate.shape
+    expert_total = local_count * size
+    turned = transposed(block)
+    held = fetched([dense_gate, dense_up])
+    if ON_CHIP:
+        turned, held = lax.optimization_barrier((turned, held))
+    arrived = gathered(turned, "tensor")
+    gain_block = lax.dynamic_slice_in_dim(gain_dense, mine_e * part, part, 0)
+    partial_sums = call(
+        dense_kernel,
+        [jax.ShapeDtypeStruct((rows, hidden), jnp.bfloat16)] * (2 * size),
+        [across[None], *arrived, gain_block[None], *map(on_chip, held)],
+        [IN_SMEM] + [IN_VMEM] * (size + 3),
+        6 << 20,
+        4 * size * rows * part * hidden,
+        4 * part * hidden,
+    )
+
+    wide = block.astype(jnp.float32)
+    squares = sum(gathered(jnp.sum(wide * wide, axis=1), "tensor"))
+    inverse = lax.rsqrt(squares / full_width + EPSILON)[:, None]
+    ids, route = pick(expert_ids, segment_index), pick(route_weights, segment_index)
+    numbers = jnp.arange(expert_total, dtype=jnp.int32)[:, None, None]
+    shares = jnp.sum(jnp.where(ids[None] == numbers, route[None], 0.0), axis=2)
+    all_shares = jnp.stack(gathered(shares, "expert"))
+    own_shares = lax.dynamic_slice_in_dim(all_shares, mine_e * local_count, local_count, 1)
+    own_shares = jnp.stack([pick(own_shares, d ^ across) for d in range(size)])
+    own_shares = jnp.swapaxes(own_shares, 1, 2)
+
+    gates, ups = partial_sums[:size], partial_sums[size:]
+    relayed = swap(ups[3], "expert", 1)
+    gate_far = swap(gates[3], "expert", 3)
+    gate_next = swap(gates[2], "expert", 2)
+    whole = swap(jnp.concatenate([gates[1], ups[1]], axis=1), "expert", 1)
+    joined = (ups[2].astype(jnp.float32) + relayed.astype(jnp.float32)).astype(jnp.bfloat16)
+    up_next = swap(joined, "expert", 2)
+    gate_sums = sum(a.astype(jnp.float32) for a in (gates[0], gate_far, gate_next, whole[:, :hidden]))
+    up_sums = sum(a.astype(jnp.float32) for a in (ups[0], up_next, whole[:, hidden:]))
+    act = jax.nn.silu(gate_sums * inverse) * (up_sums * inverse)
+    act = act.astype(jnp.bfloat16)
+
+    cut = hidden // 2
+    act_two = swap(act, "expert", 2)
+    act_far = swap(act[:, :cut], "expert", 3)
+    act_one = swap(act, "expert", 1)
+    act_rest = swap(act_two[:, cut:], "expert", 1)
+    act_three = jnp.concatenate([act_far, act_rest], axis=1)
+    acts = jnp.concatenate([act, act_one, act_two, act_three])
+    down = lax.dot_general(
+        acts, dense_down, (((1,), (1,)), ((), ())), preferred_element_type=jnp.float32
+    )
+    down = down.astype(jnp.bfloat16).reshape(size, rows, part)
+    summed = traded([pick(down, d ^ across) for d in range(size)], "tensor")
+    middle_turned = (turned.astype(jnp.float32) + summed).astype(jnp.bfloat16)
+
+    parts = jnp.stack(gathered(middle_turned, "expert"))
+    row = jnp.concatenate([pick(parts, b ^ mine_e) for b in range(size)], axis=1)
+    normed = normalize(row.astype(jnp.float32), gain_expert).astype(jnp.bfloat16)
+    experts = [expert_gate, expert_up, expert_down]
+    if ON_CHIP:
+        normed, experts = lax.optimization_barrier((normed, experts))
+    spread = gathered(normed, "tensor")
+    experts = fetched(experts)
+    columns = call(
+        expert_kernel,
+        [jax.ShapeDtypeStruct((size * rows, part), jnp.bfloat16)] * size,
+        [
+            mine_t[None],
+            *spread,
+            own_shares.reshape(size * rows, local_count),
+            *map(on_chip, experts),
+        ],
+        [IN_SMEM] + [IN_VMEM] * (size + 4),
+        12 << 20,
+        6 * size * rows * full_width * local_count * hidden_part,
+        4 * full_width * size * rows,
+    )
+    own_columns = traded(columns, "tensor").reshape(size, rows, part)
+    mixed = traded([pick(own_columns, d ^ across) for d in range(size)], "expert")
+    middle = transposed(middle_turned)
+    final = (middle.astype(jnp.float32) + mixed).astype(jnp.bfloat16)
+    other = swap(jnp.where(segment_index == 0, final, middle), "segment", 1)
+    own = jnp.where(segment_index == 0, middle, final)
+    sections = jnp.where(segment_index == 0, jnp.stack([own, other]), jnp.stack([other, own]))
+    return sections[None]
+
+
+def body(activations, expert_ids, *rest):
+    size = lax.axis_size("tensor")
+    groups = lax.axis_size("expert")
+    segments = lax.axis_size("segment")
+    expert_total = rest[4 + 2].shape[0] * groups
+    crowded = 2 * expert_ids.shape[2] >= expert_total
+    if size == groups == 4 and segments == 2 and crowded:
+        return square_body(activations, expert_ids, *rest)
+    return general_body(activations, expert_ids, *rest)
+
+
 def solution(mesh):
     placed = (
         P("segment", "expert", "tensor"),

time: 709 us -> 130 us (0.18)
  waiting for transfers between devices: 531 us -> 54.7 us
  blocking collectives: 58.7 us -> 0 us
  matrix products: 41.3 us -> 0.81 us
  starting transfers between devices: 9.73 us -> 48.2 us
  local copies, waits for them, and re-layouts: 48.6 us -> 16.2 us
  between operations: 13.9 us -> 0.35 us
  Pallas kernels: 0 us -> 7.37 us
    all_gather x5 -> x0, waiting for transfers between devices: 439 us -> none  [the longest x1 141 us: dense_folded(): lax.all_gather(dense_up, 'expert', axis=0, tiled=True)]
    unnamed x11 -> x0, waiting for transfers between devices: 77.2 us -> none
    ppermute x1 -> x36, waiting for transfers between devices: 1.25 us -> 54.7 us  [the longest x34 54.7 us: swap(): return lax.ppermute(block, axis, [(i, i ^ distance) for i in devices])]
    ppermute x1 -> x36, starting transfers between devices: 0.07 us -> 48.2 us  [the longest x34 45.9 us: swap(): return lax.ppermute(block, axis, [(i, i ^ distance) for i in devices])]
    dot_general x6 -> x1, matrix products: 41.3 us -> 0.81 us  [square_body(): lax.dot_general(acts, dense_down, (((1,), (1,)), ((), ())), preferred_ele...]
    all_to_all x2 -> x0, blocking collectives: 38.8 us -> none  [expert_block(): lax.all_to_all(outgoing, 'expert', split_axis=1, concat_axis=1, tiled=True)]
    all_to_all x2 -> x0, waiting for transfers between devices: 13.9 us -> none  [expert_block(): lax.all_to_all(summed.reshape(local_count, groups, capacity, quarter), 'e...]
    all_gather x1 -> x0, blocking collectives: 11 us -> none  [dense_prepare(): whole_rows = lax.all_gather(micro_block, 'tensor', axis=2, tiled=True)]
  transfers between devices with their start and end apart: 11 -> 36, of which waited for: 10 -> 17; matrix products, arithmetic and copies ran while one was open for 10% -> 1% of each run, Pallas kernels for 0% -> 2%
where the time goes in v2:
time: 130 us; the launch traced here: 129 us
  waiting for transfers between devices  54.7 us (42%)
  starting transfers between devices  48.2 us (37%)
  local copies, waits for them, and re-layouts  16.2 us (12%)
  Pallas kernels  7.37 us (6%)
  other arithmetic  1.87 us (1%)
    ppermute x34, waiting for transfers between devices, swap(): return lax.ppermute(block, axis, [(i, i ^ distance) for i in devices])  54.7 us
    ppermute x34, starting transfers between devices, swap(): return lax.ppermute(block, axis, [(i, i ^ distance) for i in devices])  45.9 us
    unnamed x30, local copies, waits for them, and re-layouts  15.2 us
    pallas_call x4, Pallas kernels, call(): pl.pallas_call(kernel, out_shape=out_shape, in_specs=specs, out_specs=[IN...  7.37 us
  transfers between devices with their start and end apart: 36, of which 17 were waited for; matrix products, arithmetic and copies ran while one was open for 1% of the time, Pallas kernels for 2%

profile of v2, /device:TPU:0, one launch (start us, length us, event | category | flops | bytes accessed | tf_op | source)
XLA Modules:
  0.0 129.5 jit_solution(3383271075166140804)
XLA Ops:
  0.0 1.7 %collective-permute-start = (bf16[64,640]{1,0:T(8,128)(2,1)}, bf16[64,640]{1,0:T(8,128)(2,1)S(1)}, u32[]{:S(2)}, u32[]{:S(2)}) collective-permute-start(bf16[64,640]{1,0:T(8,128)(2,1)} %bitcast.75), channel_id=1, source_target_pairs={{0,0},{1,4},{2,8},{3,12},{4,1},{5,5},{6,9},{7,13},{8,2},{9,6},{10,... | collective-permute-start | bytes 245768 | tf_op jit(solution)/shard_map/ppermute | solution.py:176
  1.7 1.5 %copy-done.4 = bf16[640,1536]{1,0:T(8,128)(2,1)S(1)} copy-done((bf16[640,1536]{1,0:T(8,128)(2,1)S(1)}, bf16[640,1536]{1,0:T(8,128)(2,1)}, u32[]{:S(2)}) %copy-start.4) | copy-done | bytes 1966104
  3.2 1.5 %copy-done.5 = bf16[640,1536]{1,0:T(8,128)(2,1)S(1)} copy-done((bf16[640,1536]{1,0:T(8,128)(2,1)S(1)}, bf16[640,1536]{1,0:T(8,128)(2,1)}, u32[]{:S(2)}) %copy-start.5) | copy-done | bytes 1966104
  8.0 7.8 %collective-permute-start.3 = (bf16[64,640]{1,0:T(8,128)(2,1)S(1)}, bf16[64,640]{1,0:T(8,128)(2,1)S(1)}, u32[]{:S(2)}, u32[]{:S(2)}) collective-permute-start(bf16[64,640]{1,0:T(8,128)(2,1)S(1)} %collective-permute-done.refs_0_), channel_id=1, source_target_pairs={{0,3},{1,2},{2,1},{3,0},{4,7},{5,6},{6,5},{7,4},{8,11},{9,10},{10,... | collective-permute-start | bytes 245768 | tf_op jit(solution)/shard_map/ppermute | solution.py:170
  16.5 3.0 %collective-permute-start.9 = (f32[64]{0:T(128)S(1)}, f32[64]{0:T(128)S(1)}, u32[]{:S(2)}, u32[]{:S(2)}) collective-permute-start(f32[64]{0:T(128)S(1)} %multiply_reduce_fusion), channel_id=1, source_target_pairs={{0,3},{1,2},{2,1},{3,0},{4,7},{5,6},{6,5},{7,4},{8,11},{9,10},{10,... | collective-permute-start | bytes 776 | tf_op jit(solution)/shard_map/ppermute | solution.py:170
  22.5 1.5 %copy-done.9 = bf16[640,1536]{1,0:T(8,128)(2,1)S(1)} copy-done((bf16[640,1536]{1,0:T(8,128)(2,1)S(1)}, bf16[640,1536]{1,0:T(8,128)(2,1)}, u32[]{:S(2)}) %copy-start.9) | copy-done | bytes 1966104
  25.4 2.7 %collective-permute-start.4 = (bf16[64,1536]{1,0:T(8,128)(2,1)S(1)}, bf16[64,1536]{1,0:T(8,128)(2,1)S(1)}, u32[]{:S(2)}, u32[]{:S(2)}) collective-permute-start(bf16[64,1536]{1,0:T(8,128)(2,1)S(1)} %get-tuple-element.35), channel_id=1, source_target_pairs={{0,12},{4,8},{8,4},{12,0},{1,13},{5,9},{9,5},{13,1},{2,14},{6,10},... | collective-permute-start | bytes 589832 | tf_op jit(solution)/shard_map/ppermute | solution.py:170
  28.1 8.4 %collective-permute-done.10 = bf16[64,1536]{1,0:T(8,128)(2,1)S(1)} collective-permute-done((bf16[64,1536]{1,0:T(8,128)(2,1)S(1)}, bf16[64,1536]{1,0:T(8,128)(2,1)S(1)}, u32[]{:S(2)}, u32[]{:S(2)}) %collective-permute-start.10) | collective-permute-done | bytes 196640 | tf_op jit(solution)/shard_map/ppermute | solution.py:170
  37.1 1.8 %collective-permute-start.5 = (bf16[64,1536]{1,0:T(8,128)(2,1)S(1)}, bf16[64,1536]{1,0:T(8,128)(2,1)S(1)}, u32[]{:S(2)}, u32[]{:S(2)}) collective-permute-start(bf16[64,1536]{1,0:T(8,128)(2,1)S(1)} %get-tuple-element.36), channel_id=1, source_target_pairs={{0,8},{4,12},{8,0},{12,4},{1,9},{5,13},{9,1},{13,5},{2,10},{6,14},... | collective-permute-start | bytes 589832 | tf_op jit(solution)/shard_map/ppermute | solution.py:170
  40.1 10.7 %collective-permute-done.5 = bf16[64,1536]{1,0:T(8,128)(2,1)S(1)} collective-permute-done((bf16[64,1536]{1,0:T(8,128)(2,1)S(1)}, bf16[64,1536]{1,0:T(8,128)(2,1)S(1)}, u32[]{:S(2)}, u32[]{:S(2)}) %collective-permute-start.5) | collective-permute-done | bytes 196640 | tf_op jit(solution)/shard_map/ppermute | solution.py:170
  50.8 5.4 %collective-permute-done.11 = bf16[64,1536]{1,0:T(8,128)(2,1)S(1)} collective-permute-done((bf16[64,1536]{1,0:T(8,128)(2,1)S(1)}, bf16[64,1536]{1,0:T(8,128)(2,1)S(1)}, u32[]{:S(2)}, u32[]{:S(2)}) %collective-permute-start.11) | collective-permute-done | bytes 196640 | tf_op jit(solution)/shard_map/ppermute | solution.py:170
  56.8 2.0 %collective-permute-start.12 = (bf16[64,1536]{1,0:T(8,128)(2,1)S(1)}, bf16[64,1536]{1,0:T(8,128)(2,1)S(1)}, u32[]{:S(2)}, u32[]{:S(2)}) collective-permute-start(bf16[64,1536]{1,0:T(8,128)(2,1)S(1)} %multiply_convert_fusion), channel_id=1, source_target_pairs={{0,4},{4,0},{8,12},{12,8},{1,5},{5,1},{9,13},{13,9},{2,6},{6,2},{1... | collective-permute-start | bytes 589832 | tf_op jit(solution)/shard_map/ppermute | solution.py:170
  58.8 2.2 %collective-permute-start.14 = (bf16[64,768]{1,0:T(8,128)(2,1)S(1)}, bf16[64,768]{1,0:T(8,128)(2,1)S(1)}, u32[]{:S(2)}, u32[]{:S(2)}) collective-permute-start(bf16[64,768]{1,0:T(8,128)(2,1)S(1)} %slice.18), channel_id=1, source_target_pairs={{0,12},{4,8},{8,4},{12,0},{1,13},{5,9},{9,5},{13,1},{2,14},{6,10},... | collective-permute-start | bytes 294920 | tf_op jit(solution)/shard_map/ppermute | solution.py:170
  61.0 7.5 %collective-permute-done.13 = bf16[64,1536]{1,0:T(8,128)(2,1)S(1)} collective-permute-done((bf16[64,1536]{1,0:T(8,128)(2,1)S(1)}, bf16[64,1536]{1,0:T(8,128)(2,1)S(1)}, u32[]{:S(2)}, u32[]{:S(2)}) %collective-permute-start.13) | collective-permute-done | bytes 196640 | tf_op jit(solution)/shard_map/ppermute | solution.py:170
  68.6 4.5 %collective-permute-done.15 = bf16[64,768]{1,0:T(8,128)(2,1)S(1)} collective-permute-done((bf16[64,768]{1,0:T(8,128)(2,1)S(1)}, bf16[64,768]{1,0:T(8,128)(2,1)S(1)}, u32[]{:S(2)}, u32[]{:S(2)}) %collective-permute-start.15) | collective-permute-done | bytes 98336 | tf_op jit(solution)/shard_map/ppermute | solution.py:170
  74.9 2.6 %collective-permute-start.17 = (bf16[64,640]{1,0:T(8,128)(2,1)S(1)}, bf16[64,640]{1,0:T(8,128)(2,1)S(1)}, u32[]{:S(2)}, u32[]{:S(2)}) collective-permute-start(bf16[64,640]{1,0:T(8,128)(2,1)S(1)} %get-tuple-element.64), channel_id=1, source_target_pairs={{0,2},{1,3},{2,0},{3,1},{4,6},{5,7},{6,4},{7,5},{8,10},{9,11},{10,... | collective-permute-start | bytes 245768 | tf_op jit(solution)/shard_map/ppermute | solution.py:170
  80.5 2.2 %collective-permute-start.22 = (bf16[64,640]{1,0:T(8,128)(2,1)S(1)}, bf16[64,640]{1,0:T(8,128)(2,1)S(1)}, u32[]{:S(2)}, u32[]{:S(2)}) collective-permute-start(bf16[64,640]{1,0:T(8,128)(2,1)S(1)} %fusion.15), channel_id=1, source_target_pairs={{0,12},{4,8},{8,4},{12,0},{1,13},{5,9},{9,5},{13,1},{2,14},{6,10},... | collective-permute-start | bytes 245768 | tf_op jit(solution)/shard_map/ppermute | solution.py:170
  82.7 2.2 %collective-permute-start.20 = (bf16[64,640]{1,0:T(8,128)(2,1)S(1)}, bf16[64,640]{1,0:T(8,128)(2,1)S(1)}, u32[]{:S(2)}, u32[]{:S(2)}) collective-permute-start(bf16[64,640]{1,0:T(8,128)(2,1)S(1)} %fusion.15), channel_id=1, source_target_pairs={{0,4},{4,0},{8,12},{12,8},{1,5},{5,1},{9,13},{13,9},{2,6},{6,2},{1... | collective-permute-start | bytes 245768 | tf_op jit(solution)/shard_map/ppermute | solution.py:170
  84.9 2.2 %collective-permute-start.28 = (f32[8,64]{1,0:T(8,128)S(1)}, f32[8,64]{1,0:T(8,128)S(1)}, u32[]{:S(2)}, u32[]{:S(2)}) collective-permute-start(f32[8,64]{1,0:T(8,128)S(1)} %select_reduce_fusion), channel_id=1, source_target_pairs={{0,12},{4,8},{8,4},{12,0},{1,13},{5,9},{9,5},{13,1},{2,14},{6,10},... | collective-permute-start | bytes 6152 | tf_op jit(solution)/shard_map/ppermute | solution.py:170
  87.1 2.2 %collective-permute-start.26 = (f32[8,64]{1,0:T(8,128)S(1)}, f32[8,64]{1,0:T(8,128)S(1)}, u32[]{:S(2)}, u32[]{:S(2)}) collective-permute-start(f32[8,64]{1,0:T(8,128)S(1)} %select_reduce_fusion), channel_id=1, source_target_pairs={{0,4},{4,0},{8,12},{12,8},{1,5},{5,1},{9,13},{13,9},{2,6},{6,2},{1... | collective-permute-start | bytes 6152 | tf_op jit(solution)/shard_map/ppermute | solution.py:170
  91.0 1.6 %collective-permute-start.24 = (bf16[64,2560]{1,0:T(8,128)(2,1)S(1)}, bf16[64,2560]{1,0:T(8,128)(2,1)S(1)}, u32[]{:S(2)}, u32[]{:S(2)}) collective-permute-start(bf16[64,2560]{1,0:T(8,128)(2,1)S(1)} %fusion.11.refs_0_), channel_id=1, source_target_pairs={{0,2},{1,3},{2,0},{3,1},{4,6},{5,7},{6,4},{7,5},{8,10},{9,11},{10,... | collective-permute-start | bytes 983048 | tf_op jit(solution)/shard_map/ppermute | solution.py:170
  93.6 2.1 %copy-done.1 = bf16[2,2560,384]{2,1,0:T(8,128)(2,1)S(1)} copy-done((bf16[2,2560,384]{2,1,0:T(8,128)(2,1)S(1)}, bf16[2,2560,384]{2,1,0:T(8,128)(2,1)}, u32[]{:S(2)}) %copy-start.1) | copy-done | bytes 3932184
  95.7 2.1 %copy-done.2 = bf16[2,2560,384]{2,1,0:T(8,128)(2,1)S(1)} copy-done((bf16[2,2560,384]{2,1,0:T(8,128)(2,1)S(1)}, bf16[2,2560,384]{2,1,0:T(8,128)(2,1)}, u32[]{:S(2)}) %copy-start.2) | copy-done | bytes 3932184
  97.8 2.1 %copy-done.3 = bf16[2,384,2560]{2,1,0:T(8,128)(2,1)S(1)} copy-done((bf16[2,384,2560]{2,1,0:T(8,128)(2,1)S(1)}, bf16[2,384,2560]{2,1,0:T(8,128)(2,1)}, u32[]{:S(2)}) %copy-start.3) | copy-done | bytes 3932184
  102.5 4.6 %shard_map.112 = (bf16[256,640]{1,0:T(8,128)(2,1)S(1)}, bf16[256,640]{1,0:T(8,128)(2,1)S(1)}, bf16[256,640]{1,0:T(8,128)(2,1)S(1)}, bf16[256,640]{1,0:T(8,128)(2,1)S(1)}) custom-call(s32[1]{0:T(128)} %bitcast.7.own_ref, bf16[64,2560]{1,0:T(8,128)(2,1)S(1)} %fusion.11.refs_0_, bf16[64,2560]{1,0:T(8,128)(2,1)S(1)} %collective-permute-done.23.refs_1_, ...), custom_call_target="tpu_custom_call" | custom-call | flops 3019898880 | bytes 2621440 | tf_op jit(solution)/shard_map/pallas_call | solution.py:208
  108.9 1.8 %collective-permute-start.31 = (bf16[256,640]{1,0:T(8,128)(2,1)S(1)}, bf16[256,640]{1,0:T(8,128)(2,1)S(1)}, u32[]{:S(2)}, u32[]{:S(2)}) collective-permute-start(bf16[256,640]{1,0:T(8,128)(2,1)S(1)} %get-tuple-element.52), channel_id=1, source_target_pairs={{0,3},{1,2},{2,1},{3,0},{4,7},{5,6},{6,5},{7,4},{8,11},{9,10},{10,... | collective-permute-start | bytes 983048 | tf_op jit(solution)/shard_map/ppermute | solution.py:170
  111.3 2.9 %collective-permute-done.29 = bf16[256,640]{1,0:T(8,128)(2,1)S(1)} collective-permute-done((bf16[256,640]{1,0:T(8,128)(2,1)S(1)}, bf16[256,640]{1,0:T(8,128)(2,1)S(1)}, u32[]{:S(2)}, u32[]{:S(2)}) %collective-permute-start.29) | collective-permute-done | bytes 327712 | tf_op jit(solution)/shard_map/ppermute | solution.py:170
  114.7 3.9 %collective-permute-done.31 = bf16[256,640]{1,0:T(8,128)(2,1)S(1)} collective-permute-done((bf16[256,640]{1,0:T(8,128)(2,1)S(1)}, bf16[256,640]{1,0:T(8,128)(2,1)S(1)}, u32[]{:S(2)}, u32[]{:S(2)}) %collective-permute-start.31) | collective-permute-done | bytes 327712 | tf_op jit(solution)/shard_map/ppermute | solution.py:170
  118.9 1.7 %collective-permute-start.34 = (bf16[64,640]{1,0:T(8,128)(2,1)S(1)}, bf16[64,640]{1,0:T(8,128)(2,1)S(1)}, u32[]{:S(2)}, u32[]{:S(2)}) collective-permute-start(bf16[64,640]{1,0:T(8,128)(2,1)S(1)} %get-tuple-element.56), channel_id=1, source_target_pairs={{0,12},{4,8},{8,4},{12,0},{1,13},{5,9},{9,5},{13,1},{2,14},{6,10},... | collective-permute-start | bytes 245768 | tf_op jit(solution)/shard_map/ppermute | solution.py:170
  120.5 1.8 %collective-permute-start.33 = (bf16[64,640]{1,0:T(8,128)(2,1)S(1)}, bf16[64,640]{1,0:T(8,128)(2,1)S(1)}, u32[]{:S(2)}, u32[]{:S(2)}) collective-permute-start(bf16[64,640]{1,0:T(8,128)(2,1)S(1)} %get-tuple-element.57), channel_id=1, source_target_pairs={{0,8},{4,12},{8,0},{12,4},{1,9},{5,13},{9,1},{13,5},{2,10},{6,14},... | collective-permute-start | bytes 245768 | tf_op jit(solution)/shard_map/ppermute | solution.py:170
  123.3 2.0 %collective-permute-done.34 = bf16[64,640]{1,0:T(8,128)(2,1)S(1)} collective-permute-done((bf16[64,640]{1,0:T(8,128)(2,1)S(1)}, bf16[64,640]{1,0:T(8,128)(2,1)S(1)}, u32[]{:S(2)}, u32[]{:S(2)}) %collective-permute-start.34) | collective-permute-done | bytes 81952 | tf_op jit(solution)/shard_map/ppermute | solution.py:170
  125.3 2.1 %collective-permute-done.33 = bf16[64,640]{1,0:T(8,128)(2,1)S(1)} collective-permute-done((bf16[64,640]{1,0:T(8,128)(2,1)S(1)}, bf16[64,640]{1,0:T(8,128)(2,1)S(1)}, u32[]{:S(2)}, u32[]{:S(2)}) %collective-permute-start.33) | collective-permute-done | bytes 81952 | tf_op jit(solution)/shard_map/ppermute | solution.py:170
  (103 shorter events, 26.6 us)
Async XLA Ops:
  0.0 8.0 %collective-permute-start = (bf16[64,640]{1,0:T(8,128)(2,1)}, bf16[64,640]{1,0:T(8,128)(2,1)S(1)}, u32[]{:S(2)}, u32[]{:S(2)}) collective-permute-start(bf16[64,640]{1,0:T(8,128)(2,1)} %bitcast.75), channel_id=1, source_target_pairs={{0,0},{1,4},{2,8},{3,12},{4,1},{5,5},{6,9},{7,13},{8,2},{9,6},{10,... | collective-permute-start | bytes 245768 | tf_op jit(solution)/shard_map/ppermute | solution.py:176
  8.0 12.3 %collective-permute-start.3 = (bf16[64,640]{1,0:T(8,128)(2,1)S(1)}, bf16[64,640]{1,0:T(8,128)(2,1)S(1)}, u32[]{:S(2)}, u32[]{:S(2)}) collective-permute-start(bf16[64,640]{1,0:T(8,128)(2,1)S(1)} %collective-permute-done.refs_0_), channel_id=1, source_target_pairs={{0,3},{1,2},{2,1},{3,0},{4,7},{5,6},{6,5},{7,4},{8,11},{9,10},{10,... | collective-permute-start | bytes 245768 | tf_op jit(solution)/shard_map/ppermute | solution.py:170
  15.8 5.1 %collective-permute-start.2 = (bf16[64,640]{1,0:T(8,128)(2,1)S(1)}, bf16[64,640]{1,0:T(8,128)(2,1)S(1)}, u32[]{:S(2)}, u32[]{:S(2)}) collective-permute-start(bf16[64,640]{1,0:T(8,128)(2,1)S(1)} %collective-permute-done.refs_0_), channel_id=1, source_target_pairs={{0,2},{1,3},{2,0},{3,1},{4,6},{5,7},{6,4},{7,5},{8,10},{9,11},{10,... | collective-permute-start | bytes 245768 | tf_op jit(solution)/shard_map/ppermute | solution.py:170
  15.8 5.1 %collective-permute-start.1 = (bf16[64,640]{1,0:T(8,128)(2,1)S(1)}, bf16[64,640]{1,0:T(8,128)(2,1)S(1)}, u32[]{:S(2)}, u32[]{:S(2)}) collective-permute-start(bf16[64,640]{1,0:T(8,128)(2,1)S(1)} %collective-permute-done.refs_0_), channel_id=1, source_target_pairs={{0,1},{1,0},{2,3},{3,2},{4,5},{5,4},{6,7},{7,6},{8,9},{9,8},{10,11... | collective-permute-start | bytes 245768 | tf_op jit(solution)/shard_map/ppermute | solution.py:170
  16.5 20.6 %collective-permute-start.9 = (f32[64]{0:T(128)S(1)}, f32[64]{0:T(128)S(1)}, u32[]{:S(2)}, u32[]{:S(2)}) collective-permute-start(f32[64]{0:T(128)S(1)} %multiply_reduce_fusion), channel_id=1, source_target_pairs={{0,3},{1,2},{2,1},{3,0},{4,7},{5,6},{6,5},{7,4},{8,11},{9,10},{10,... | collective-permute-start | bytes 776 | tf_op jit(solution)/shard_map/ppermute | solution.py:170
  19.5 19.4 %collective-permute-start.8 = (f32[64]{0:T(128)S(1)}, f32[64]{0:T(128)S(1)}, u32[]{:S(2)}, u32[]{:S(2)}) collective-permute-start(f32[64]{0:T(128)S(1)} %multiply_reduce_fusion), channel_id=1, source_target_pairs={{0,2},{1,3},{2,0},{3,1},{4,6},{5,7},{6,4},{7,5},{8,10},{9,11},{10,... | collective-permute-start | bytes 776 | tf_op jit(solution)/shard_map/ppermute | solution.py:170
  20.3 19.8 %collective-permute-start.7 = (f32[64]{0:T(128)S(1)}, f32[64]{0:T(128)S(1)}, u32[]{:S(2)}, u32[]{:S(2)}) collective-permute-start(f32[64]{0:T(128)S(1)} %multiply_reduce_fusion), channel_id=1, source_target_pairs={{0,1},{1,0},{2,3},{3,2},{4,5},{5,4},{6,7},{7,6},{8,9},{9,8},{10,11... | collective-permute-start | bytes 776 | tf_op jit(solution)/shard_map/ppermute | solution.py:170
  25.4 14.6 %collective-permute-start.4 = (bf16[64,1536]{1,0:T(8,128)(2,1)S(1)}, bf16[64,1536]{1,0:T(8,128)(2,1)S(1)}, u32[]{:S(2)}, u32[]{:S(2)}) collective-permute-start(bf16[64,1536]{1,0:T(8,128)(2,1)S(1)} %get-tuple-element.35), channel_id=1, source_target_pairs={{0,12},{4,8},{8,4},{12,0},{1,13},{5,9},{9,5},{13,1},{2,14},{6,10},... | collective-permute-start | bytes 589832 | tf_op jit(solution)/shard_map/ppermute | solution.py:170
  28.1 8.5 %collective-permute-start.10 = (bf16[64,1536]{1,0:T(8,128)(2,1)S(1)}, bf16[64,1536]{1,0:T(8,128)(2,1)S(1)}, u32[]{:S(2)}, u32[]{:S(2)}) collective-permute-start(bf16[64,1536]{1,0:T(8,128)(2,1)S(1)} %get-tuple-element.41), channel_id=1, source_target_pairs={{0,4},{4,0},{8,12},{12,8},{1,5},{5,1},{9,13},{13,9},{2,6},{6,2},{1... | collective-permute-start | bytes 589832 | tf_op jit(solution)/shard_map/ppermute | solution.py:170
  36.6 19.6 %collective-permute-start.6 = (bf16[64,3072]{1,0:T(8,128)(2,1)S(1)}, bf16[64,3072]{1,0:T(8,128)(2,1)S(1)}, u32[]{:S(2)}, u32[]{:S(2)}) collective-permute-start(bf16[64,3072]{1,0:T(8,128)(2,1)S(1)} %pad_maximum_fusion), channel_id=1, source_target_pairs={{0,4},{4,0},{8,12},{12,8},{1,5},{5,1},{9,13},{13,9},{2,6},{6,2},{1... | collective-permute-start | bytes 1179656 | tf_op jit(solution)/shard_map/ppermute | solution.py:170
  37.1 13.7 %collective-permute-start.5 = (bf16[64,1536]{1,0:T(8,128)(2,1)S(1)}, bf16[64,1536]{1,0:T(8,128)(2,1)S(1)}, u32[]{:S(2)}, u32[]{:S(2)}) collective-permute-start(bf16[64,1536]{1,0:T(8,128)(2,1)S(1)} %get-tuple-element.36), channel_id=1, source_target_pairs={{0,8},{4,12},{8,0},{12,4},{1,9},{5,13},{9,1},{13,5},{2,10},{6,14},... | collective-permute-start | bytes 589832 | tf_op jit(solution)/shard_map/ppermute | solution.py:170
  38.9 17.3 %collective-permute-start.11 = (bf16[64,1536]{1,0:T(8,128)(2,1)S(1)}, bf16[64,1536]{1,0:T(8,128)(2,1)S(1)}, u32[]{:S(2)}, u32[]{:S(2)}) collective-permute-start(bf16[64,1536]{1,0:T(8,128)(2,1)S(1)} %add_convert_fusion), channel_id=1, source_target_pairs={{0,8},{4,12},{8,0},{12,4},{1,9},{5,13},{9,1},{13,5},{2,10},{6,14},... | collective-permute-start | bytes 589832 | tf_op jit(solution)/shard_map/ppermute | solution.py:170
  56.5 12.0 %collective-permute-start.13 = (bf16[64,1536]{1,0:T(8,128)(2,1)S(1)}, bf16[64,1536]{1,0:T(8,128)(2,1)S(1)}, u32[]{:S(2)}, u32[]{:S(2)}) collective-permute-start(bf16[64,1536]{1,0:T(8,128)(2,1)S(1)} %multiply_convert_fusion), channel_id=1, source_target_pairs={{0,8},{4,12},{8,0},{12,4},{1,9},{5,13},{9,1},{13,5},{2,10},{6,14},... | collective-permute-start | bytes 589832 | tf_op jit(solution)/shard_map/ppermute | solution.py:170
  56.8 11.9 %collective-permute-start.12 = (bf16[64,1536]{1,0:T(8,128)(2,1)S(1)}, bf16[64,1536]{1,0:T(8,128)(2,1)S(1)}, u32[]{:S(2)}, u32[]{:S(2)}) collective-permute-start(bf16[64,1536]{1,0:T(8,128)(2,1)S(1)} %multiply_convert_fusion), channel_id=1, source_target_pairs={{0,4},{4,0},{8,12},{12,8},{1,5},{5,1},{9,13},{13,9},{2,6},{6,2},{1... | collective-permute-start | bytes 589832 | tf_op jit(solution)/shard_map/ppermute | solution.py:170
  58.8 9.8 %collective-permute-start.14 = (bf16[64,768]{1,0:T(8,128)(2,1)S(1)}, bf16[64,768]{1,0:T(8,128)(2,1)S(1)}, u32[]{:S(2)}, u32[]{:S(2)}) collective-permute-start(bf16[64,768]{1,0:T(8,128)(2,1)S(1)} %slice.18), channel_id=1, source_target_pairs={{0,12},{4,8},{8,4},{12,0},{1,13},{5,9},{9,5},{13,1},{2,14},{6,10},... | collective-permute-start | bytes 294920 | tf_op jit(solution)/shard_map/ppermute | solution.py:170
  74.1 5.4 %collective-permute-start.18 = (bf16[64,640]{1,0:T(8,128)(2,1)S(1)}, bf16[64,640]{1,0:T(8,128)(2,1)S(1)}, u32[]{:S(2)}, u32[]{:S(2)}) collective-permute-start(bf16[64,640]{1,0:T(8,128)(2,1)S(1)} %get-tuple-element.63), channel_id=1, source_target_pairs={{0,3},{1,2},{2,1},{3,0},{4,7},{5,6},{6,5},{7,4},{8,11},{9,10},{10,... | collective-permute-start | bytes 245768 | tf_op jit(solution)/shard_map/ppermute | solution.py:170
  74.9 5.5 %collective-permute-start.17 = (bf16[64,640]{1,0:T(8,128)(2,1)S(1)}, bf16[64,640]{1,0:T(8,128)(2,1)S(1)}, u32[]{:S(2)}, u32[]{:S(2)}) collective-permute-start(bf16[64,640]{1,0:T(8,128)(2,1)S(1)} %get-tuple-element.64), channel_id=1, source_target_pairs={{0,2},{1,3},{2,0},{3,1},{4,6},{5,7},{6,4},{7,5},{8,10},{9,11},{10,... | collective-permute-start | bytes 245768 | tf_op jit(solution)/shard_map/ppermute | solution.py:170
  80.5 6.7 %collective-permute-start.22 = (bf16[64,640]{1,0:T(8,128)(2,1)S(1)}, bf16[64,640]{1,0:T(8,128)(2,1)S(1)}, u32[]{:S(2)}, u32[]{:S(2)}) collective-permute-start(bf16[64,640]{1,0:T(8,128)(2,1)S(1)} %fusion.15), channel_id=1, source_target_pairs={{0,12},{4,8},{8,4},{12,0},{1,13},{5,9},{9,5},{13,1},{2,14},{6,10},... | collective-permute-start | bytes 245768 | tf_op jit(solution)/shard_map/ppermute | solution.py:170
  82.7 6.7 %collective-permute-start.21 = (bf16[64,640]{1,0:T(8,128)(2,1)S(1)}, bf16[64,640]{1,0:T(8,128)(2,1)S(1)}, u32[]{:S(2)}, u32[]{:S(2)}) collective-permute-start(bf16[64,640]{1,0:T(8,128)(2,1)S(1)} %fusion.15), channel_id=1, source_target_pairs={{0,8},{4,12},{8,0},{12,4},{1,9},{5,13},{9,1},{13,5},{2,10},{6,14},... | collective-permute-start | bytes 245768 | tf_op jit(solution)/shard_map/ppermute | solution.py:170
  82.7 6.7 %collective-permute-start.20 = (bf16[64,640]{1,0:T(8,128)(2,1)S(1)}, bf16[64,640]{1,0:T(8,128)(2,1)S(1)}, u32[]{:S(2)}, u32[]{:S(2)}) collective-permute-start(bf16[64,640]{1,0:T(8,128)(2,1)S(1)} %fusion.15), channel_id=1, source_target_pairs={{0,4},{4,0},{8,12},{12,8},{1,5},{5,1},{9,13},{13,9},{2,6},{6,2},{1... | collective-permute-start | bytes 245768 | tf_op jit(solution)/shard_map/ppermute | solution.py:170
  84.9 7.8 %collective-permute-start.28 = (f32[8,64]{1,0:T(8,128)S(1)}, f32[8,64]{1,0:T(8,128)S(1)}, u32[]{:S(2)}, u32[]{:S(2)}) collective-permute-start(f32[8,64]{1,0:T(8,128)S(1)} %select_reduce_fusion), channel_id=1, source_target_pairs={{0,12},{4,8},{8,4},{12,0},{1,13},{5,9},{9,5},{13,1},{2,14},{6,10},... | collective-permute-start | bytes 6152 | tf_op jit(solution)/shard_map/ppermute | solution.py:170
  87.1 6.3 %collective-permute-start.27 = (f32[8,64]{1,0:T(8,128)S(1)}, f32[8,64]{1,0:T(8,128)S(1)}, u32[]{:S(2)}, u32[]{:S(2)}) collective-permute-start(f32[8,64]{1,0:T(8,128)S(1)} %select_reduce_fusion), channel_id=1, source_target_pairs={{0,8},{4,12},{8,0},{12,4},{1,9},{5,13},{9,1},{13,5},{2,10},{6,14},... | collective-permute-start | bytes 6152 | tf_op jit(solution)/shard_map/ppermute | solution.py:170
  87.1 6.2 %collective-permute-start.26 = (f32[8,64]{1,0:T(8,128)S(1)}, f32[8,64]{1,0:T(8,128)S(1)}, u32[]{:S(2)}, u32[]{:S(2)}) collective-permute-start(f32[8,64]{1,0:T(8,128)S(1)} %select_reduce_fusion), channel_id=1, source_target_pairs={{0,4},{4,0},{8,12},{12,8},{1,5},{5,1},{9,13},{13,9},{2,6},{6,2},{1... | collective-permute-start | bytes 6152 | tf_op jit(solution)/shard_map/ppermute | solution.py:170
  89.8 10.9 %collective-permute-start.25 = (bf16[64,2560]{1,0:T(8,128)(2,1)S(1)}, bf16[64,2560]{1,0:T(8,128)(2,1)S(1)}, u32[]{:S(2)}, u32[]{:S(2)}) collective-permute-start(bf16[64,2560]{1,0:T(8,128)(2,1)S(1)} %fusion.11.refs_0_), channel_id=1, source_target_pairs={{0,3},{1,2},{2,1},{3,0},{4,7},{5,6},{6,5},{7,4},{8,11},{9,10},{10,... | collective-permute-start | bytes 983048 | tf_op jit(solution)/shard_map/ppermute | solution.py:170
  91.0 10.5 %collective-permute-start.24 = (bf16[64,2560]{1,0:T(8,128)(2,1)S(1)}, bf16[64,2560]{1,0:T(8,128)(2,1)S(1)}, u32[]{:S(2)}, u32[]{:S(2)}) collective-permute-start(bf16[64,2560]{1,0:T(8,128)(2,1)S(1)} %fusion.11.refs_0_), channel_id=1, source_target_pairs={{0,2},{1,3},{2,0},{3,1},{4,6},{5,7},{6,4},{7,5},{8,10},{9,11},{10,... | collective-permute-start | bytes 983048 | tf_op jit(solution)/shard_map/ppermute | solution.py:170
  92.7 9.8 %collective-permute-start.23 = (bf16[64,2560]{1,0:T(8,128)(2,1)S(1)}, bf16[64,2560]{1,0:T(8,128)(2,1)S(1)}, u32[]{:S(2)}, u32[]{:S(2)}) collective-permute-start(bf16[64,2560]{1,0:T(8,128)(2,1)S(1)} %fusion.11.refs_0_), channel_id=1, source_target_pairs={{0,1},{1,0},{2,3},{3,2},{4,5},{5,4},{6,7},{7,6},{8,9},{9,8},{10,11... | collective-permute-start | bytes 983048 | tf_op jit(solution)/shard_map/ppermute | solution.py:170
  107.1 7.1 %collective-permute-start.29 = (bf16[256,640]{1,0:T(8,128)(2,1)S(1)}, bf16[256,640]{1,0:T(8,128)(2,1)S(1)}, u32[]{:S(2)}, u32[]{:S(2)}) collective-permute-start(bf16[256,640]{1,0:T(8,128)(2,1)S(1)} %get-tuple-element.50), channel_id=1, source_target_pairs={{0,1},{1,0},{2,3},{3,2},{4,5},{5,4},{6,7},{7,6},{8,9},{9,8},{10,11... | collective-permute-start | bytes 983048 | tf_op jit(solution)/shard_map/ppermute | solution.py:170
  107.6 7.1 %collective-permute-start.30 = (bf16[256,640]{1,0:T(8,128)(2,1)S(1)}, bf16[256,640]{1,0:T(8,128)(2,1)S(1)}, u32[]{:S(2)}, u32[]{:S(2)}) collective-permute-start(bf16[256,640]{1,0:T(8,128)(2,1)S(1)} %get-tuple-element.51), channel_id=1, source_target_pairs={{0,2},{1,3},{2,0},{3,1},{4,6},{5,7},{6,4},{7,5},{8,10},{9,11},{10,... | collective-permute-start | bytes 983048 | tf_op jit(solution)/shard_map/ppermute | solution.py:170
  108.9 9.7 %collective-permute-start.31 = (bf16[256,640]{1,0:T(8,128)(2,1)S(1)}, bf16[256,640]{1,0:T(8,128)(2,1)S(1)}, u32[]{:S(2)}, u32[]{:S(2)}) collective-permute-start(bf16[256,640]{1,0:T(8,128)(2,1)S(1)} %get-tuple-element.52), channel_id=1, source_target_pairs={{0,3},{1,2},{2,1},{3,0},{4,7},{5,6},{6,5},{7,4},{8,11},{9,10},{10,... | collective-permute-start | bytes 983048 | tf_op jit(solution)/shard_map/ppermute | solution.py:170
  110.6 11.7 %collective-permute-start.19 = (bf16[64,640]{1,0:T(8,128)(2,1)S(1)}, bf16[64,640]{1,0:T(8,128)(2,1)S(1)}, u32[]{:S(2)}, u32[]{:S(2)}) collective-permute-start(bf16[64,640]{1,0:T(8,128)(2,1)S(1)} %fusion.15), channel_id=1, source_target_pairs={{0,0},{1,4},{2,8},{3,12},{4,1},{5,5},{6,9},{7,13},{8,2},{9,6},{10,... | collective-permute-start | bytes 245768 | tf_op jit(solution)/shard_map/ppermute | solution.py:176
  118.9 6.4 %collective-permute-start.34 = (bf16[64,640]{1,0:T(8,128)(2,1)S(1)}, bf16[64,640]{1,0:T(8,128)(2,1)S(1)}, u32[]{:S(2)}, u32[]{:S(2)}) collective-permute-start(bf16[64,640]{1,0:T(8,128)(2,1)S(1)} %get-tuple-element.56), channel_id=1, source_target_pairs={{0,12},{4,8},{8,4},{12,0},{1,13},{5,9},{9,5},{13,1},{2,14},{6,10},... | collective-permute-start | bytes 245768 | tf_op jit(solution)/shard_map/ppermute | solution.py:170
  120.5 6.8 %collective-permute-start.33 = (bf16[64,640]{1,0:T(8,128)(2,1)S(1)}, bf16[64,640]{1,0:T(8,128)(2,1)S(1)}, u32[]{:S(2)}, u32[]{:S(2)}) collective-permute-start(bf16[64,640]{1,0:T(8,128)(2,1)S(1)} %get-tuple-element.57), channel_id=1, source_target_pairs={{0,8},{4,12},{8,0},{12,4},{1,9},{5,13},{9,1},{13,5},{2,10},{6,14},... | collective-permute-start | bytes 245768 | tf_op jit(solution)/shard_map/ppermute | solution.py:170
  (18 other events, 182.8 us)

commit v3 on v2

--- a/solution.py
+++ b/solution.py
@@ -244,14 +244,14 @@
     )
 
 
-def dense_kernel(across_ref, *refs):
+def dense_kernel(place_ref, *refs):
     size = lax.axis_size("tensor")
     blocks, (gain_ref, *weights), outs = refs[:size], refs[size : size + 3], refs[size + 3 :]
     hidden = weights[0].shape[1]
     step = hidden // STEPS
-    across = across_ref[0]
-    gain = gain_ref[...]
-    rows = blocks[0].shape[0]
+    across = place_ref[0]
+    rows, part = blocks[0].shape
+    gain = gain_ref[:, pl.ds(pl.multiple_of(place_ref[1] * part, LANES), part)]
     scaled = []
     for d in range(size):
         block = blocks[d][...]
@@ -315,16 +315,21 @@
     if ON_CHIP:
         turned, held = lax.optimization_barrier((turned, held))
     arrived = gathered(turned, "tensor")
-    gain_block = lax.dynamic_slice_in_dim(gain_dense, mine_e * part, part, 0)
     partial_sums = call(
         dense_kernel,
         [jax.ShapeDtypeStruct((rows, hidden), jnp.bfloat16)] * (2 * size),
-        [across[None], *arrived, gain_block[None], *map(on_chip, held)],
+        [jnp.stack([across, mine_e]), *arrived, gain_dense[None], *map(on_chip, held)],
         [IN_SMEM] + [IN_VMEM] * (size + 3),
         6 << 20,
         4 * size * rows * part * hidden,
         4 * part * hidden,
     )
+
+    if ON_CHIP:
+        first, expert_ids, route_weights = lax.optimization_barrier(
+            (partial_sums[0], expert_ids, route_weights)
+        )
+        partial_sums = [first, *partial_sums[1:]]
 
     wide = block.astype(jnp.float32)
     squares = sum(gathered(jnp.sum(wide * wide, axis=1), "tensor"))
@@ -349,12 +354,9 @@
     act = jax.nn.silu(gate_sums * inverse) * (up_sums * inverse)
     act = act.astype(jnp.bfloat16)
 
-    cut = hidden // 2
     act_two = swap(act, "expert", 2)
-    act_far = swap(act[:, :cut], "expert", 3)
     act_one = swap(act, "expert", 1)
-    act_rest = swap(act_two[:, cut:], "expert", 1)
-    act_three = jnp.concatenate([act_far, act_rest], axis=1)
+    act_three = swap(act_two, "expert", 1)
     acts = jnp.concatenate([act, act_one, act_two, act_three])
     down = lax.dot_general(
         acts, dense_down, (((1,), (1,)), ((), ())), preferred_element_type=jnp.float32

time: 130 us -> 130 us (level)
  local copies, waits for them, and re-layouts: 16.2 us -> 10.4 us
  waiting for transfers between devices: 54.7 us -> 60.1 us
    unnamed x30 -> x18, local copies, waits for them, and re-layouts: 15.2 us -> 9.45 us
    ppermute x34 -> x33, waiting for transfers between devices: 54.7 us -> 60.1 us  [swap(): return lax.ppermute(block, axis, [(i, i ^ distance) for i in devices])]
    ppermute x34 -> x33, starting transfers between devices: 45.9 us -> 45.3 us  [swap(): return lax.ppermute(block, axis, [(i, i ^ distance) for i in devices])]
  transfers between devices with their start and end apart: 36 -> 35, of which waited for: 17 -> 19; matrix products, arithmetic and copies ran while one was open for 1% -> 2% of each run, Pallas kernels for 2% -> 3%
where the time goes in v3:
time: 130 us
  waiting for transfers between devices  60.1 us (46%)
  starting transfers between devices  47.6 us (37%)
  local copies, waits for them, and re-layouts  10.4 us (8%)
  Pallas kernels  7.91 us (6%)
  other arithmetic  2.83 us (2%)
    ppermute x33, waiting for transfers between devices, swap(): return lax.ppermute(block, axis, [(i, i ^ distance) for i in devices])  60.1 us
    ppermute x33, starting transfers between devices, swap(): return lax.ppermute(block, axis, [(i, i ^ distance) for i in devices])  45.3 us
    unnamed x18, local copies, waits for them, and re-layouts  9.45 us
    pallas_call x4, Pallas kernels, call(): pl.pallas_call(kernel, out_shape=out_shape, in_specs=specs, out_specs=[IN...  7.91 us
  transfers between devices with their start and end apart: 35, of which 19 were waited for; matrix products, arithmetic and copies ran while one was open for 2% of the time, Pallas kernels for 3%

profile of v3, /device:TPU:0, one launch (start us, length us, event | category | flops | bytes accessed | tf_op | source)
XLA Modules:
  0.0 129.9 jit_solution(1200299213966920991)
XLA Ops:
  0.0 1.7 %collective-permute-start = (bf16[64,640]{1,0:T(8,128)(2,1)}, bf16[64,640]{1,0:T(8,128)(2,1)S(1)}, u32[]{:S(2)}, u32[]{:S(2)}) collective-permute-start(bf16[64,640]{1,0:T(8,128)(2,1)} %bitcast.74), channel_id=1, source_target_pairs={{0,0},{1,4},{2,8},{3,12},{4,1},{5,5},{6,9},{7,13},{8,2},{9,6},{10,... | collective-permute-start | bytes 245768 | tf_op jit(solution)/shard_map/ppermute | solution.py:176
  2.7 7.9 %collective-permute-start.9 = (f32[64]{0:T(128)S(1)}, f32[64]{0:T(128)S(1)}, u32[]{:S(2)}, u32[]{:S(2)}) collective-permute-start(f32[64]{0:T(128)S(1)} %multiply_reduce_fusion), channel_id=1, source_target_pairs={{0,3},{1,2},{2,1},{3,0},{4,7},{5,6},{6,5},{7,4},{8,11},{9,10},{10,... | collective-permute-start | bytes 776 | tf_op jit(solution)/shard_map/ppermute | solution.py:170
  11.3 1.5 %copy-done.4 = bf16[640,1536]{1,0:T(8,128)(2,1)S(1)} copy-done((bf16[640,1536]{1,0:T(8,128)(2,1)S(1)}, bf16[640,1536]{1,0:T(8,128)(2,1)}, u32[]{:S(2)}) %copy-start.4) | copy-done | bytes 1966104
  12.8 1.5 %copy-done.5 = bf16[640,1536]{1,0:T(8,128)(2,1)S(1)} copy-done((bf16[640,1536]{1,0:T(8,128)(2,1)S(1)}, bf16[640,1536]{1,0:T(8,128)(2,1)}, u32[]{:S(2)}) %copy-start.5) | copy-done | bytes 1966104
  18.6 2.5 %collective-permute-done.3.refs_3_ = bf16[64,640]{1,0:T(8,128)(2,1)S(1)} collective-permute-done((bf16[64,640]{1,0:T(8,128)(2,1)S(1)}, bf16[64,640]{1,0:T(8,128)(2,1)S(1)}, u32[]{:S(2)}, u32[]{:S(2)}) %collective-permute-start.3) | collective-permute-done | bytes 81952 | tf_op jit(solution)/shard_map/ppermute | solution.py:170
  21.8 1.9 %shard_map.110 = (bf16[64,1536]{1,0:T(8,128)(2,1)S(1)}, bf16[64,1536]{1,0:T(8,128)(2,1)S(1)}, bf16[64,1536]{1,0:T(8,128)(2,1)S(1)}, bf16[64,1536]{1,0:T(8,128)(2...) custom-call(s32[2]{0:T(128)S(1)} %pad_add_fusion.place_ref, ...), custom_call_target="tpu_custom_call" | custom-call | flops 1006632960 | bytes 3932160 | tf_op jit(solution)/shard_map/pallas_call | solution.py:208
  23.8 2.4 %collective-permute-start.4 = (bf16[64,1536]{1,0:T(8,128)(2,1)S(1)}, bf16[64,1536]{1,0:T(8,128)(2,1)S(1)}, u32[]{:S(2)}, u32[]{:S(2)}) collective-permute-start(bf16[64,1536]{1,0:T(8,128)(2,1)S(1)} %get-tuple-element.39), channel_id=1, source_target_pairs={{0,12},{4,8},{8,4},{12,0},{1,13},{5,9},{9,5},{13,1},{2,14},{6,10},... | collective-permute-start | bytes 589832 | tf_op jit(solution)/shard_map/ppermute | solution.py:170
  26.3 8.7 %collective-permute-done.10 = bf16[64,1536]{1,0:T(8,128)(2,1)S(1)} collective-permute-done((bf16[64,1536]{1,0:T(8,128)(2,1)S(1)}, bf16[64,1536]{1,0:T(8,128)(2,1)S(1)}, u32[]{:S(2)}, u32[]{:S(2)}) %collective-permute-start.10) | collective-permute-done | bytes 196640 | tf_op jit(solution)/shard_map/ppermute | solution.py:170
  35.4 1.8 %collective-permute-start.5 = (bf16[64,1536]{1,0:T(8,128)(2,1)S(1)}, bf16[64,1536]{1,0:T(8,128)(2,1)S(1)}, u32[]{:S(2)}, u32[]{:S(2)}) collective-permute-start(bf16[64,1536]{1,0:T(8,128)(2,1)S(1)} %get-tuple-element.40), channel_id=1, source_target_pairs={{0,8},{4,12},{8,0},{12,4},{1,9},{5,13},{9,1},{13,5},{2,10},{6,14},... | collective-permute-start | bytes 589832 | tf_op jit(solution)/shard_map/ppermute | solution.py:170
  38.5 10.7 %collective-permute-done.5 = bf16[64,1536]{1,0:T(8,128)(2,1)S(1)} collective-permute-done((bf16[64,1536]{1,0:T(8,128)(2,1)S(1)}, bf16[64,1536]{1,0:T(8,128)(2,1)S(1)}, u32[]{:S(2)}, u32[]{:S(2)}) %collective-permute-start.5) | collective-permute-done | bytes 196640 | tf_op jit(solution)/shard_map/ppermute | solution.py:170
  49.1 5.5 %collective-permute-done.11 = bf16[64,1536]{1,0:T(8,128)(2,1)S(1)} collective-permute-done((bf16[64,1536]{1,0:T(8,128)(2,1)S(1)}, bf16[64,1536]{1,0:T(8,128)(2,1)S(1)}, u32[]{:S(2)}, u32[]{:S(2)}) %collective-permute-start.11) | collective-permute-done | bytes 196640 | tf_op jit(solution)/shard_map/ppermute | solution.py:170
  55.2 1.9 %collective-permute-start.12 = (bf16[64,1536]{1,0:T(8,128)(2,1)S(1)}, bf16[64,1536]{1,0:T(8,128)(2,1)S(1)}, u32[]{:S(2)}, u32[]{:S(2)}) collective-permute-start(bf16[64,1536]{1,0:T(8,128)(2,1)S(1)} %multiply_convert_fusion), channel_id=1, source_target_pairs={{0,4},{4,0},{8,12},{12,8},{1,5},{5,1},{9,13},{13,9},{2,6},{6,2},{1... | collective-permute-start | bytes 589832 | tf_op jit(solution)/shard_map/ppermute | solution.py:170
  57.2 6.6 %collective-permute-done.13 = bf16[64,1536]{1,0:T(8,128)(2,1)S(1)} collective-permute-done((bf16[64,1536]{1,0:T(8,128)(2,1)S(1)}, bf16[64,1536]{1,0:T(8,128)(2,1)S(1)}, u32[]{:S(2)}, u32[]{:S(2)}) %collective-permute-start.13) | collective-permute-done | bytes 196640 | tf_op jit(solution)/shard_map/ppermute | solution.py:170
  63.9 5.5 %collective-permute-done.14 = bf16[64,1536]{1,0:T(8,128)(2,1)S(1)} collective-permute-done((bf16[64,1536]{1,0:T(8,128)(2,1)S(1)}, bf16[64,1536]{1,0:T(8,128)(2,1)S(1)}, u32[]{:S(2)}, u32[]{:S(2)}) %collective-permute-start.14) | collective-permute-done | bytes 196640 | tf_op jit(solution)/shard_map/ppermute | solution.py:170
  71.3 2.1 %collective-permute-start.17 = (bf16[64,640]{1,0:T(8,128)(2,1)S(1)}, bf16[64,640]{1,0:T(8,128)(2,1)S(1)}, u32[]{:S(2)}, u32[]{:S(2)}) collective-permute-start(bf16[64,640]{1,0:T(8,128)(2,1)S(1)} %get-tuple-element.69), channel_id=1, source_target_pairs={{0,3},{1,2},{2,1},{3,0},{4,7},{5,6},{6,5},{7,4},{8,11},{9,10},{10,... | collective-permute-start | bytes 245768 | tf_op jit(solution)/shard_map/ppermute | solution.py:170
  74.8 1.9 %collective-permute-done.17 = bf16[64,640]{1,0:T(8,128)(2,1)S(1)} collective-permute-done((bf16[64,640]{1,0:T(8,128)(2,1)S(1)}, bf16[64,640]{1,0:T(8,128)(2,1)S(1)}, u32[]{:S(2)}, u32[]{:S(2)}) %collective-permute-start.17) | collective-permute-done | bytes 81952 | tf_op jit(solution)/shard_map/ppermute | solution.py:170
  77.9 2.4 %collective-permute-start.21 = (bf16[64,640]{1,0:T(8,128)(2,1)S(1)}, bf16[64,640]{1,0:T(8,128)(2,1)S(1)}, u32[]{:S(2)}, u32[]{:S(2)}) collective-permute-start(bf16[64,640]{1,0:T(8,128)(2,1)S(1)} %fusion.13), channel_id=1, source_target_pairs={{0,12},{4,8},{8,4},{12,0},{1,13},{5,9},{9,5},{13,1},{2,14},{6,10},... | collective-permute-start | bytes 245768 | tf_op jit(solution)/shard_map/ppermute | solution.py:170
  80.3 2.1 %collective-permute-start.19 = (bf16[64,640]{1,0:T(8,128)(2,1)S(1)}, bf16[64,640]{1,0:T(8,128)(2,1)S(1)}, u32[]{:S(2)}, u32[]{:S(2)}) collective-permute-start(bf16[64,640]{1,0:T(8,128)(2,1)S(1)} %fusion.13), channel_id=1, source_target_pairs={{0,4},{4,0},{8,12},{12,8},{1,5},{5,1},{9,13},{13,9},{2,6},{6,2},{1... | collective-permute-start | bytes 245768 | tf_op jit(solution)/shard_map/ppermute | solution.py:170
  82.4 2.4 %collective-permute-start.27 = (f32[8,64]{1,0:T(8,128)S(1)}, f32[8,64]{1,0:T(8,128)S(1)}, u32[]{:S(2)}, u32[]{:S(2)}) collective-permute-start(f32[8,64]{1,0:T(8,128)S(1)} %select_reduce_fusion), channel_id=1, source_target_pairs={{0,12},{4,8},{8,4},{12,0},{1,13},{5,9},{9,5},{13,1},{2,14},{6,10},... | collective-permute-start | bytes 6152 | tf_op jit(solution)/shard_map/ppermute | solution.py:170
  84.7 2.1 %collective-permute-start.25 = (f32[8,64]{1,0:T(8,128)S(1)}, f32[8,64]{1,0:T(8,128)S(1)}, u32[]{:S(2)}, u32[]{:S(2)}) collective-permute-start(f32[8,64]{1,0:T(8,128)S(1)} %select_reduce_fusion), channel_id=1, source_target_pairs={{0,4},{4,0},{8,12},{12,8},{1,5},{5,1},{9,13},{13,9},{2,6},{6,2},{1... | collective-permute-start | bytes 6152 | tf_op jit(solution)/shard_map/ppermute | solution.py:170
  87.3 1.8 %collective-permute-start.24 = (bf16[64,2560]{1,0:T(8,128)(2,1)S(1)}, bf16[64,2560]{1,0:T(8,128)(2,1)S(1)}, u32[]{:S(2)}, u32[]{:S(2)}) collective-permute-start(bf16[64,2560]{1,0:T(8,128)(2,1)S(1)} %fusion.9.refs_0_), channel_id=1, source_target_pairs={{0,3},{1,2},{2,1},{3,0},{4,7},{5,6},{6,5},{7,4},{8,11},{9,10},{10,... | collective-permute-start | bytes 983048 | tf_op jit(solution)/shard_map/ppermute | solution.py:170
  91.0 2.1 %copy-done.1 = bf16[2,2560,384]{2,1,0:T(8,128)(2,1)S(1)} copy-done((bf16[2,2560,384]{2,1,0:T(8,128)(2,1)S(1)}, bf16[2,2560,384]{2,1,0:T(8,128)(2,1)}, u32[]{:S(2)}) %copy-start.1) | copy-done | bytes 3932184
  93.1 2.1 %copy-done.2 = bf16[2,2560,384]{2,1,0:T(8,128)(2,1)S(1)} copy-done((bf16[2,2560,384]{2,1,0:T(8,128)(2,1)S(1)}, bf16[2,2560,384]{2,1,0:T(8,128)(2,1)}, u32[]{:S(2)}) %copy-start.2) | copy-done | bytes 3932184
  95.2 2.1 %copy-done.3 = bf16[2,384,2560]{2,1,0:T(8,128)(2,1)S(1)} copy-done((bf16[2,384,2560]{2,1,0:T(8,128)(2,1)S(1)}, bf16[2,384,2560]{2,1,0:T(8,128)(2,1)}, u32[]{:S(2)}) %copy-start.3) | copy-done | bytes 3932184
  99.2 4.6 %shard_map.112 = (bf16[256,640]{1,0:T(8,128)(2,1)S(1)}, bf16[256,640]{1,0:T(8,128)(2,1)S(1)}, bf16[256,640]{1,0:T(8,128)(2,1)S(1)}, bf16[256,640]{1,0:T(8,128)(2,1)S(1)}) custom-call(s32[1]{0:T(128)} %bitcast.8.own_ref, bf16[64,2560]{1,0:T(8,128)(2,1)S(1)} %fusion.9.refs_0_, bf16[64,2560]{1,0:T(8,128)(2,1)S(1)} %collective-permute-done.22.refs_1_, ...), custom_call_target="tpu_custom_call" | custom-call | flops 3019898880 | bytes 2621440 | tf_op jit(solution)/shard_map/pallas_call | solution.py:208
  105.8 1.6 %collective-permute-start.30 = (bf16[256,640]{1,0:T(8,128)(2,1)S(1)}, bf16[256,640]{1,0:T(8,128)(2,1)S(1)}, u32[]{:S(2)}, u32[]{:S(2)}) collective-permute-start(bf16[256,640]{1,0:T(8,128)(2,1)S(1)} %get-tuple-element.58), channel_id=1, source_target_pairs={{0,3},{1,2},{2,1},{3,0},{4,7},{5,6},{6,5},{7,4},{8,11},{9,10},{10,... | collective-permute-start | bytes 983048 | tf_op jit(solution)/shard_map/ppermute | solution.py:170
  108.0 2.9 %collective-permute-done.28 = bf16[256,640]{1,0:T(8,128)(2,1)S(1)} collective-permute-done((bf16[256,640]{1,0:T(8,128)(2,1)S(1)}, bf16[256,640]{1,0:T(8,128)(2,1)S(1)}, u32[]{:S(2)}, u32[]{:S(2)}) %collective-permute-start.28) | collective-permute-done | bytes 327712 | tf_op jit(solution)/shard_map/ppermute | solution.py:170
  111.0 4.2 %collective-permute-done.29 = bf16[256,640]{1,0:T(8,128)(2,1)S(1)} collective-permute-done((bf16[256,640]{1,0:T(8,128)(2,1)S(1)}, bf16[256,640]{1,0:T(8,128)(2,1)S(1)}, u32[]{:S(2)}, u32[]{:S(2)}) %collective-permute-start.29) | collective-permute-done | bytes 327712 | tf_op jit(solution)/shard_map/ppermute | solution.py:170
  116.3 2.1 %collective-permute-start.31 = (bf16[64,640]{1,0:T(8,128)(2,1)S(1)}, bf16[64,640]{1,0:T(8,128)(2,1)S(1)}, u32[]{:S(2)}, u32[]{:S(2)}) collective-permute-start(bf16[64,640]{1,0:T(8,128)(2,1)S(1)} %get-tuple-element.61), channel_id=1, source_target_pairs={{0,4},{4,0},{8,12},{12,8},{1,5},{5,1},{9,13},{13,9},{2,6},{6,2},{1... | collective-permute-start | bytes 245768 | tf_op jit(solution)/shard_map/ppermute | solution.py:170
  118.4 4.1 %collective-permute-start.33 = (bf16[64,640]{1,0:T(8,128)(2,1)S(1)}, bf16[64,640]{1,0:T(8,128)(2,1)S(1)}, u32[]{:S(2)}, u32[]{:S(2)}) collective-permute-start(bf16[64,640]{1,0:T(8,128)(2,1)S(1)} %get-tuple-element.62), channel_id=1, source_target_pairs={{0,12},{4,8},{8,4},{12,0},{1,13},{5,9},{9,5},{13,1},{2,14},{6,10},... | collective-permute-start | bytes 245768 | tf_op jit(solution)/shard_map/ppermute | solution.py:170
  122.5 3.3 %collective-permute-done.33 = bf16[64,640]{1,0:T(8,128)(2,1)S(1)} collective-permute-done((bf16[64,640]{1,0:T(8,128)(2,1)S(1)}, bf16[64,640]{1,0:T(8,128)(2,1)S(1)}, u32[]{:S(2)}, u32[]{:S(2)}) %collective-permute-start.33) | collective-permute-done | bytes 81952 | tf_op jit(solution)/shard_map/ppermute | solution.py:170
  125.8 2.0 %collective-permute-done.32 = bf16[64,640]{1,0:T(8,128)(2,1)S(1)} collective-permute-done((bf16[64,640]{1,0:T(8,128)(2,1)S(1)}, bf16[64,640]{1,0:T(8,128)(2,1)S(1)}, u32[]{:S(2)}, u32[]{:S(2)}) %collective-permute-start.32) | collective-permute-done | bytes 81952 | tf_op jit(solution)/shard_map/ppermute | solution.py:170
  (89 shorter events, 23.7 us)
Async XLA Ops:
  0.0 15.0 %collective-permute-start = (bf16[64,640]{1,0:T(8,128)(2,1)}, bf16[64,640]{1,0:T(8,128)(2,1)S(1)}, u32[]{:S(2)}, u32[]{:S(2)}) collective-permute-start(bf16[64,640]{1,0:T(8,128)(2,1)} %bitcast.74), channel_id=1, source_target_pairs={{0,0},{1,4},{2,8},{3,12},{4,1},{5,5},{6,9},{7,13},{8,2},{9,6},{10,... | collective-permute-start | bytes 245768 | tf_op jit(solution)/shard_map/ppermute | solution.py:176
  2.7 32.8 %collective-permute-start.9 = (f32[64]{0:T(128)S(1)}, f32[64]{0:T(128)S(1)}, u32[]{:S(2)}, u32[]{:S(2)}) collective-permute-start(f32[64]{0:T(128)S(1)} %multiply_reduce_fusion), channel_id=1, source_target_pairs={{0,3},{1,2},{2,1},{3,0},{4,7},{5,6},{6,5},{7,4},{8,11},{9,10},{10,... | collective-permute-start | bytes 776 | tf_op jit(solution)/shard_map/ppermute | solution.py:170
  10.6 26.7 %collective-permute-start.8 = (f32[64]{0:T(128)S(1)}, f32[64]{0:T(128)S(1)}, u32[]{:S(2)}, u32[]{:S(2)}) collective-permute-start(f32[64]{0:T(128)S(1)} %multiply_reduce_fusion), channel_id=1, source_target_pairs={{0,2},{1,3},{2,0},{3,1},{4,6},{5,7},{6,4},{7,5},{8,10},{9,11},{10,... | collective-permute-start | bytes 776 | tf_op jit(solution)/shard_map/ppermute | solution.py:170
  15.0 6.2 %collective-permute-start.3 = (bf16[64,640]{1,0:T(8,128)(2,1)S(1)}, bf16[64,640]{1,0:T(8,128)(2,1)S(1)}, u32[]{:S(2)}, u32[]{:S(2)}) collective-permute-start(bf16[64,640]{1,0:T(8,128)(2,1)S(1)} %collective-permute-done.refs_0_), channel_id=1, source_target_pairs={{0,3},{1,2},{2,1},{3,0},{4,7},{5,6},{6,5},{7,4},{8,11},{9,10},{10,... | collective-permute-start | bytes 245768 | tf_op jit(solution)/shard_map/ppermute | solution.py:170
  16.1 5.3 %collective-permute-start.2 = (bf16[64,640]{1,0:T(8,128)(2,1)S(1)}, bf16[64,640]{1,0:T(8,128)(2,1)S(1)}, u32[]{:S(2)}, u32[]{:S(2)}) collective-permute-start(bf16[64,640]{1,0:T(8,128)(2,1)S(1)} %collective-permute-done.refs_0_), channel_id=1, source_target_pairs={{0,2},{1,3},{2,0},{3,1},{4,6},{5,7},{6,4},{7,5},{8,10},{9,11},{10,... | collective-permute-start | bytes 245768 | tf_op jit(solution)/shard_map/ppermute | solution.py:170
  17.2 4.7 %collective-permute-start.1 = (bf16[64,640]{1,0:T(8,128)(2,1)S(1)}, bf16[64,640]{1,0:T(8,128)(2,1)S(1)}, u32[]{:S(2)}, u32[]{:S(2)}) collective-permute-start(bf16[64,640]{1,0:T(8,128)(2,1)S(1)} %collective-permute-done.refs_0_), channel_id=1, source_target_pairs={{0,1},{1,0},{2,3},{3,2},{4,5},{5,4},{6,7},{7,6},{8,9},{9,8},{10,11... | collective-permute-start | bytes 245768 | tf_op jit(solution)/shard_map/ppermute | solution.py:170
  21.1 17.3 %collective-permute-start.7 = (f32[64]{0:T(128)S(1)}, f32[64]{0:T(128)S(1)}, u32[]{:S(2)}, u32[]{:S(2)}) collective-permute-start(f32[64]{0:T(128)S(1)} %multiply_reduce_fusion), channel_id=1, source_target_pairs={{0,1},{1,0},{2,3},{3,2},{4,5},{5,4},{6,7},{7,6},{8,9},{9,8},{10,11... | collective-permute-start | bytes 776 | tf_op jit(solution)/shard_map/ppermute | solution.py:170
  23.8 14.7 %collective-permute-start.4 = (bf16[64,1536]{1,0:T(8,128)(2,1)S(1)}, bf16[64,1536]{1,0:T(8,128)(2,1)S(1)}, u32[]{:S(2)}, u32[]{:S(2)}) collective-permute-start(bf16[64,1536]{1,0:T(8,128)(2,1)S(1)} %get-tuple-element.39), channel_id=1, source_target_pairs={{0,12},{4,8},{8,4},{12,0},{1,13},{5,9},{9,5},{13,1},{2,14},{6,10},... | collective-permute-start | bytes 589832 | tf_op jit(solution)/shard_map/ppermute | solution.py:170
  26.2 8.7 %collective-permute-start.10 = (bf16[64,1536]{1,0:T(8,128)(2,1)S(1)}, bf16[64,1536]{1,0:T(8,128)(2,1)S(1)}, u32[]{:S(2)}, u32[]{:S(2)}) collective-permute-start(bf16[64,1536]{1,0:T(8,128)(2,1)S(1)} %get-tuple-element.45), channel_id=1, source_target_pairs={{0,4},{4,0},{8,12},{12,8},{1,5},{5,1},{9,13},{13,9},{2,6},{6,2},{1... | collective-permute-start | bytes 589832 | tf_op jit(solution)/shard_map/ppermute | solution.py:170
  34.9 19.7 %collective-permute-start.6 = (bf16[64,3072]{1,0:T(8,128)(2,1)S(1)}, bf16[64,3072]{1,0:T(8,128)(2,1)S(1)}, u32[]{:S(2)}, u32[]{:S(2)}) collective-permute-start(bf16[64,3072]{1,0:T(8,128)(2,1)S(1)} %pad_maximum_fusion), channel_id=1, source_target_pairs={{0,4},{4,0},{8,12},{12,8},{1,5},{5,1},{9,13},{13,9},{2,6},{6,2},{1... | collective-permute-start | bytes 1179656 | tf_op jit(solution)/shard_map/ppermute | solution.py:170
  35.4 13.7 %collective-permute-start.5 = (bf16[64,1536]{1,0:T(8,128)(2,1)S(1)}, bf16[64,1536]{1,0:T(8,128)(2,1)S(1)}, u32[]{:S(2)}, u32[]{:S(2)}) collective-permute-start(bf16[64,1536]{1,0:T(8,128)(2,1)S(1)} %get-tuple-element.40), channel_id=1, source_target_pairs={{0,8},{4,12},{8,0},{12,4},{1,9},{5,13},{9,1},{13,5},{2,10},{6,14},... | collective-permute-start | bytes 589832 | tf_op jit(solution)/shard_map/ppermute | solution.py:170
  37.3 17.4 %collective-permute-start.11 = (bf16[64,1536]{1,0:T(8,128)(2,1)S(1)}, bf16[64,1536]{1,0:T(8,128)(2,1)S(1)}, u32[]{:S(2)}, u32[]{:S(2)}) collective-permute-start(bf16[64,1536]{1,0:T(8,128)(2,1)S(1)} %add_convert_fusion), channel_id=1, source_target_pairs={{0,8},{4,12},{8,0},{12,4},{1,9},{5,13},{9,1},{13,5},{2,10},{6,14},... | collective-permute-start | bytes 589832 | tf_op jit(solution)/shard_map/ppermute | solution.py:170
  55.0 8.8 %collective-permute-start.13 = (bf16[64,1536]{1,0:T(8,128)(2,1)S(1)}, bf16[64,1536]{1,0:T(8,128)(2,1)S(1)}, u32[]{:S(2)}, u32[]{:S(2)}) collective-permute-start(bf16[64,1536]{1,0:T(8,128)(2,1)S(1)} %multiply_convert_fusion), channel_id=1, source_target_pairs={{0,8},{4,12},{8,0},{12,4},{1,9},{5,13},{9,1},{13,5},{2,10},{6,14},... | collective-permute-start | bytes 589832 | tf_op jit(solution)/shard_map/ppermute | solution.py:170
  55.2 8.7 %collective-permute-start.12 = (bf16[64,1536]{1,0:T(8,128)(2,1)S(1)}, bf16[64,1536]{1,0:T(8,128)(2,1)S(1)}, u32[]{:S(2)}, u32[]{:S(2)}) collective-permute-start(bf16[64,1536]{1,0:T(8,128)(2,1)S(1)} %multiply_convert_fusion), channel_id=1, source_target_pairs={{0,4},{4,0},{8,12},{12,8},{1,5},{5,1},{9,13},{13,9},{2,6},{6,2},{1... | collective-permute-start | bytes 589832 | tf_op jit(solution)/shard_map/ppermute | solution.py:170
  63.7 5.7 %collective-permute-start.14 = (bf16[64,1536]{1,0:T(8,128)(2,1)S(1)}, bf16[64,1536]{1,0:T(8,128)(2,1)S(1)}, u32[]{:S(2)}, u32[]{:S(2)}) collective-permute-start(bf16[64,1536]{1,0:T(8,128)(2,1)S(1)} %collective-permute-done.13), channel_id=1, source_target_pairs={{0,4},{4,0},{8,12},{12,8},{1,5},{5,1},{9,13},{13,9},{2,6},{6,2},{1... | collective-permute-start | bytes 589832 | tf_op jit(solution)/shard_map/ppermute | solution.py:170
  71.3 5.4 %collective-permute-start.17 = (bf16[64,640]{1,0:T(8,128)(2,1)S(1)}, bf16[64,640]{1,0:T(8,128)(2,1)S(1)}, u32[]{:S(2)}, u32[]{:S(2)}) collective-permute-start(bf16[64,640]{1,0:T(8,128)(2,1)S(1)} %get-tuple-element.69), channel_id=1, source_target_pairs={{0,3},{1,2},{2,1},{3,0},{4,7},{5,6},{6,5},{7,4},{8,11},{9,10},{10,... | collective-permute-start | bytes 245768 | tf_op jit(solution)/shard_map/ppermute | solution.py:170
  77.9 6.9 %collective-permute-start.21 = (bf16[64,640]{1,0:T(8,128)(2,1)S(1)}, bf16[64,640]{1,0:T(8,128)(2,1)S(1)}, u32[]{:S(2)}, u32[]{:S(2)}) collective-permute-start(bf16[64,640]{1,0:T(8,128)(2,1)S(1)} %fusion.13), channel_id=1, source_target_pairs={{0,12},{4,8},{8,4},{12,0},{1,13},{5,9},{9,5},{13,1},{2,14},{6,10},... | collective-permute-start | bytes 245768 | tf_op jit(solution)/shard_map/ppermute | solution.py:170
  80.3 6.5 %collective-permute-start.20 = (bf16[64,640]{1,0:T(8,128)(2,1)S(1)}, bf16[64,640]{1,0:T(8,128)(2,1)S(1)}, u32[]{:S(2)}, u32[]{:S(2)}) collective-permute-start(bf16[64,640]{1,0:T(8,128)(2,1)S(1)} %fusion.13), channel_id=1, source_target_pairs={{0,8},{4,12},{8,0},{12,4},{1,9},{5,13},{9,1},{13,5},{2,10},{6,14},... | collective-permute-start | bytes 245768 | tf_op jit(solution)/shard_map/ppermute | solution.py:170
  80.3 6.5 %collective-permute-start.19 = (bf16[64,640]{1,0:T(8,128)(2,1)S(1)}, bf16[64,640]{1,0:T(8,128)(2,1)S(1)}, u32[]{:S(2)}, u32[]{:S(2)}) collective-permute-start(bf16[64,640]{1,0:T(8,128)(2,1)S(1)} %fusion.13), channel_id=1, source_target_pairs={{0,4},{4,0},{8,12},{12,8},{1,5},{5,1},{9,13},{13,9},{2,6},{6,2},{1... | collective-permute-start | bytes 245768 | tf_op jit(solution)/shard_map/ppermute | solution.py:170
  82.4 7.2 %collective-permute-start.27 = (f32[8,64]{1,0:T(8,128)S(1)}, f32[8,64]{1,0:T(8,128)S(1)}, u32[]{:S(2)}, u32[]{:S(2)}) collective-permute-start(f32[8,64]{1,0:T(8,128)S(1)} %select_reduce_fusion), channel_id=1, source_target_pairs={{0,12},{4,8},{8,4},{12,0},{1,13},{5,9},{9,5},{13,1},{2,14},{6,10},... | collective-permute-start | bytes 6152 | tf_op jit(solution)/shard_map/ppermute | solution.py:170
  84.7 6.1 %collective-permute-start.26 = (f32[8,64]{1,0:T(8,128)S(1)}, f32[8,64]{1,0:T(8,128)S(1)}, u32[]{:S(2)}, u32[]{:S(2)}) collective-permute-start(f32[8,64]{1,0:T(8,128)S(1)} %select_reduce_fusion), channel_id=1, source_target_pairs={{0,8},{4,12},{8,0},{12,4},{1,9},{5,13},{9,1},{13,5},{2,10},{6,14},... | collective-permute-start | bytes 6152 | tf_op jit(solution)/shard_map/ppermute | solution.py:170
  84.7 6.1 %collective-permute-start.25 = (f32[8,64]{1,0:T(8,128)S(1)}, f32[8,64]{1,0:T(8,128)S(1)}, u32[]{:S(2)}, u32[]{:S(2)}) collective-permute-start(f32[8,64]{1,0:T(8,128)S(1)} %select_reduce_fusion), channel_id=1, source_target_pairs={{0,4},{4,0},{8,12},{12,8},{1,5},{5,1},{9,13},{13,9},{2,6},{6,2},{1... | collective-permute-start | bytes 6152 | tf_op jit(solution)/shard_map/ppermute | solution.py:170
  87.3 10.9 %collective-permute-start.24 = (bf16[64,2560]{1,0:T(8,128)(2,1)S(1)}, bf16[64,2560]{1,0:T(8,128)(2,1)S(1)}, u32[]{:S(2)}, u32[]{:S(2)}) collective-permute-start(bf16[64,2560]{1,0:T(8,128)(2,1)S(1)} %fusion.9.refs_0_), channel_id=1, source_target_pairs={{0,3},{1,2},{2,1},{3,0},{4,7},{5,6},{6,5},{7,4},{8,11},{9,10},{10,... | collective-permute-start | bytes 983048 | tf_op jit(solution)/shard_map/ppermute | solution.py:170
  89.1 10.2 %collective-permute-start.23 = (bf16[64,2560]{1,0:T(8,128)(2,1)S(1)}, bf16[64,2560]{1,0:T(8,128)(2,1)S(1)}, u32[]{:S(2)}, u32[]{:S(2)}) collective-permute-start(bf16[64,2560]{1,0:T(8,128)(2,1)S(1)} %fusion.9.refs_0_), channel_id=1, source_target_pairs={{0,2},{1,3},{2,0},{3,1},{4,6},{5,7},{6,4},{7,5},{8,10},{9,11},{10,... | collective-permute-start | bytes 983048 | tf_op jit(solution)/shard_map/ppermute | solution.py:170
  89.6 9.7 %collective-permute-start.22 = (bf16[64,2560]{1,0:T(8,128)(2,1)S(1)}, bf16[64,2560]{1,0:T(8,128)(2,1)S(1)}, u32[]{:S(2)}, u32[]{:S(2)}) collective-permute-start(bf16[64,2560]{1,0:T(8,128)(2,1)S(1)} %fusion.9.refs_0_), channel_id=1, source_target_pairs={{0,1},{1,0},{2,3},{3,2},{4,5},{5,4},{6,7},{7,6},{8,9},{9,8},{10,11... | collective-permute-start | bytes 983048 | tf_op jit(solution)/shard_map/ppermute | solution.py:170
  103.8 7.1 %collective-permute-start.28 = (bf16[256,640]{1,0:T(8,128)(2,1)S(1)}, bf16[256,640]{1,0:T(8,128)(2,1)S(1)}, u32[]{:S(2)}, u32[]{:S(2)}) collective-permute-start(bf16[256,640]{1,0:T(8,128)(2,1)S(1)} %get-tuple-element.56), channel_id=1, source_target_pairs={{0,1},{1,0},{2,3},{3,2},{4,5},{5,4},{6,7},{7,6},{8,9},{9,8},{10,11... | collective-permute-start | bytes 983048 | tf_op jit(solution)/shard_map/ppermute | solution.py:170
  104.5 10.6 %collective-permute-start.29 = (bf16[256,640]{1,0:T(8,128)(2,1)S(1)}, bf16[256,640]{1,0:T(8,128)(2,1)S(1)}, u32[]{:S(2)}, u32[]{:S(2)}) collective-permute-start(bf16[256,640]{1,0:T(8,128)(2,1)S(1)} %get-tuple-element.57), channel_id=1, source_target_pairs={{0,2},{1,3},{2,0},{3,1},{4,6},{5,7},{6,4},{7,5},{8,10},{9,11},{10,... | collective-permute-start | bytes 983048 | tf_op jit(solution)/shard_map/ppermute | solution.py:170
  105.8 10.4 %collective-permute-start.30 = (bf16[256,640]{1,0:T(8,128)(2,1)S(1)}, bf16[256,640]{1,0:T(8,128)(2,1)S(1)}, u32[]{:S(2)}, u32[]{:S(2)}) collective-permute-start(bf16[256,640]{1,0:T(8,128)(2,1)S(1)} %get-tuple-element.58), channel_id=1, source_target_pairs={{0,3},{1,2},{2,1},{3,0},{4,7},{5,6},{6,5},{7,4},{8,11},{9,10},{10,... | collective-permute-start | bytes 983048 | tf_op jit(solution)/shard_map/ppermute | solution.py:170
  107.4 15.1 %collective-permute-start.18 = (bf16[64,640]{1,0:T(8,128)(2,1)S(1)}, bf16[64,640]{1,0:T(8,128)(2,1)S(1)}, u32[]{:S(2)}, u32[]{:S(2)}) collective-permute-start(bf16[64,640]{1,0:T(8,128)(2,1)S(1)} %fusion.13), channel_id=1, source_target_pairs={{0,0},{1,4},{2,8},{3,12},{4,1},{5,5},{6,9},{7,13},{8,2},{9,6},{10,... | collective-permute-start | bytes 245768 | tf_op jit(solution)/shard_map/ppermute | solution.py:176
  116.3 6.2 %collective-permute-start.31 = (bf16[64,640]{1,0:T(8,128)(2,1)S(1)}, bf16[64,640]{1,0:T(8,128)(2,1)S(1)}, u32[]{:S(2)}, u32[]{:S(2)}) collective-permute-start(bf16[64,640]{1,0:T(8,128)(2,1)S(1)} %get-tuple-element.61), channel_id=1, source_target_pairs={{0,4},{4,0},{8,12},{12,8},{1,5},{5,1},{9,13},{13,9},{2,6},{6,2},{1... | collective-permute-start | bytes 245768 | tf_op jit(solution)/shard_map/ppermute | solution.py:170
  118.4 7.4 %collective-permute-start.33 = (bf16[64,640]{1,0:T(8,128)(2,1)S(1)}, bf16[64,640]{1,0:T(8,128)(2,1)S(1)}, u32[]{:S(2)}, u32[]{:S(2)}) collective-permute-start(bf16[64,640]{1,0:T(8,128)(2,1)S(1)} %get-tuple-element.62), channel_id=1, source_target_pairs={{0,12},{4,8},{8,4},{12,0},{1,13},{5,9},{9,5},{13,1},{2,14},{6,10},... | collective-permute-start | bytes 245768 | tf_op jit(solution)/shard_map/ppermute | solution.py:170
  122.5 5.3 %collective-permute-start.32 = (bf16[64,640]{1,0:T(8,128)(2,1)S(1)}, bf16[64,640]{1,0:T(8,128)(2,1)S(1)}, u32[]{:S(2)}, u32[]{:S(2)}) collective-permute-start(bf16[64,640]{1,0:T(8,128)(2,1)S(1)} %get-tuple-element.63), channel_id=1, source_target_pairs={{0,8},{4,12},{8,0},{12,4},{1,9},{5,13},{9,1},{13,5},{2,10},{6,14},... | collective-permute-start | bytes 245768 | tf_op jit(solution)/shard_map/ppermute | solution.py:170
  (12 other events, 186.0 us)
